TPU v7x, 32 devices: a whole 2x2x4 slice. The times are simulated.
32 devices in a mesh: groups: 2 (over y), seq: 4 (over z), dp: 4 (over x, core).
Axes of the slice: x: 2, y: 2, z: 4, core: 2. Of those that a mesh axis runs over, the one named last changes fastest.
Arguments:
- inputs: bfloat16 [8, 4096, 448], P(('groups', 'dp'), 'seq'), parts along dimension 0, may hold values from -6 to 6
- cotangent: bfloat16 [8, 4096, 448], P(('groups', 'dp'), 'seq'), parts along dimension 0, may hold values from -6 to 6
- first_weight_matrix: bfloat16 [3, 448, 448], P(None, None, 'dp'), may hold values from -0.15625 to 0.15625
- weight_two: bfloat16 [3, 448, 448], P(None, None, 'dp'), may hold values from -0.15625 to 0.15625
Outputs:
- input_grad: bfloat16 [8, 4096, 448], P(('groups', 'dp'), 'seq'), parts along dimension 0
- grad_one: float32 [6, 448, 448], P('groups', None, 'dp'), parts along dimension 0
- grad_two: float32 [6, 448, 448], P('groups', None, 'dp'), parts along dimension 0
There are 2 independent parts, one for each index of `groups`. A program takes and returns all parts, laid end to end along the dimension named above; an argument that names none is the same for every part. Nothing has to cross between parts.
All inputs are finite; a program needn't handle non-finite values.
Results may differ from a plain program's by a relative error of at most 0.012.
Values may be sent and summed in bfloat16 or wider, within the bound.
No kernel may reach another device: no remote copies, remote signals or barrier semaphores. Data moves between devices by JAX's collectives and lax.ppermute only.
A program may use at most 64 MiB of HBM per device.

v0:
```python
import math

import jax
import jax.numpy as jnp
from jax import lax
from jax.sharding import PartitionSpec as P


def shifted(block, axis, distance):
    devices = range(lax.axis_size(axis))
    route = [(i - distance, i) for i in devices if i - distance in devices]
    return lax.ppermute(block, axis, route)


def gelu_slope(value):
    return jax.vjp(jax.nn.gelu, value)[1](jnp.ones_like(value))[0]


def outer_terms(left, right, factor):
    product = lax.dot_general(
        left, right, (((0,), (0,)), ((), ())), preferred_element_type=jnp.float32
    )
    return product * factor


def back_product(tap, weight):
    return lax.dot_general(
        tap, weight, (((1,), (1,)), ((), ())), preferred_element_type=jnp.float32
    )


def on_device(inputs, cotangent, first_weight_matrix, weight_two):
    chans = inputs.shape[2]
    rows = inputs.shape[0] * inputs.shape[1]
    factor = 1.0 / math.sqrt(
        inputs.shape[0] * lax.axis_size("dp") * inputs.shape[1] * lax.axis_size("seq")
    )
    full_one = lax.all_gather(first_weight_matrix, "dp", axis=2, tiled=True)
    flat_in = inputs.reshape(rows, chans)
    inputs_f = flat_in.astype(jnp.float32)
    input_activation = jax.nn.gelu(inputs_f).astype(jnp.bfloat16)
    act_before = shifted(input_activation, "seq", 2)
    act_after = shifted(input_activation, "seq", -2)
    flat_cot = cotangent.reshape(rows, chans)
    cot_later = shifted(flat_cot, "seq", -4)
    cot_earlier = shifted(flat_cot, "seq", 4)
    preactivation = jnp.dot(act_before, full_one[0], preferred_element_type=jnp.float32)
    preactivation = preactivation + jnp.dot(
        input_activation, full_one[1], preferred_element_type=jnp.float32
    )
    preactivation = preactivation + jnp.dot(
        act_after, full_one[2], preferred_element_type=jnp.float32
    )
    hidden_f = (inputs_f + preactivation).astype(jnp.bfloat16).astype(jnp.float32)
    act_one = jax.nn.gelu(hidden_f).astype(jnp.bfloat16)
    full_two = lax.all_gather(weight_two, "dp", axis=2, tiled=True)
    second_layer_taps = (cot_later, flat_cot, cot_earlier)
    delta_one = back_product(second_layer_taps[0], full_two[0])
    delta_one = delta_one + back_product(second_layer_taps[1], full_two[1])
    delta_one = delta_one + back_product(second_layer_taps[2], full_two[2])
    middle_gradient = (flat_cot.astype(jnp.float32) + gelu_slope(hidden_f) * delta_one).astype(
        jnp.bfloat16
    )
    part_two = jnp.stack(
        [outer_terms(act_one, second_layer_taps[k], factor) for k in range(3)]
    ).astype(jnp.bfloat16)
    grad_two = lax.psum(
        lax.psum_scatter(part_two, "dp", scatter_dimension=2, tiled=True).astype(jnp.float32), "seq"
    )
    grad_later = shifted(middle_gradient, "seq", -2)
    grad_earlier = shifted(middle_gradient, "seq", 2)
    first_layer_taps = (grad_later, middle_gradient, grad_earlier)
    delta_zero = back_product(first_layer_taps[0], full_one[0])
    delta_zero = delta_zero + back_product(first_layer_taps[1], full_one[1])
    delta_zero = delta_zero + back_product(first_layer_taps[2], full_one[2])
    input_grad = (middle_gradient.astype(jnp.float32) + gelu_slope(inputs_f) * delta_zero).astype(
        jnp.bfloat16
    )
    part_one = jnp.stack(
        [outer_terms(input_activation, first_layer_taps[k], factor) for k in range(3)]
    ).astype(jnp.bfloat16)
    grad_one = lax.psum(
        lax.psum_scatter(part_one, "dp", scatter_dimension=2, tiled=True).astype(jnp.float32), "seq"
    )
    return (input_grad.reshape(inputs.shape), grad_one, grad_two)


def solution(mesh):
    placed = (
        P(("groups", "dp"), "seq", None),
        P(("groups", "dp"), "seq", None),
        P(None, None, "dp"),
        P(None, None, "dp"),
    )
    return jax.shard_map(
        on_device,
        mesh=mesh,
        in_specs=placed,
        out_specs=(
            P(("groups", "dp"), "seq", None),
            P("groups", None, "dp"),
            P("groups", None, "dp"),
        ),
        check_vma=False,
    )
```

profile of v0, /device:TPU:0, one launch (start us, length us, event | category | flops | bytes accessed | tf_op | source)
XLA Modules:
  0.0 242.5 jit_solution(234301999639612765)
XLA Ops:
  7.2 0.0 all-gather.3.cloned.1.call-start
  7.2 2.2 copy.9
  9.4 0.0 all-gather.3.cloned.1.call-update
  9.4 0.0 all-gather.5.cloned.1.call-start
  9.5 2.1 copy.13
  11.6 0.0 all-gather.5.cloned.1.call-update
  11.6 0.0 reduce-scatter.9.cloned.1.call-start
  11.7 1.6 fusion.26
  13.2 6.9 %collective-permute-start = (bf16[1024,448]{0,1:T(8,128)(2,1)}, bf16[1024,448]{0,1:T(8,128)(2,1)}, u32[]{:S(2)}, u32[]{:S(2)}) collective-permute-start(bf16[1024,448]{0,1:T(8,128)(2,1)} %fusion.26), channel_id=1, source_target_pairs={{0,8},{4,12},{1,9},{5,13},{2,10},{6,14},{3,11},{7,15},{16,24},{20,... | collective-permute-start | bytes 2752520 | tf_op jit(solution)/shard_map/ppermute | solution.py:12
  20.1 1.3 collective-permute-start.1
  21.4 1.6 collective-permute-start.2
  23.0 11.0 %all-gather.3.cloned.1.call-done = bf16[3,448,448]{1,0,2:T(4,128)(2,1)} async-done(((bf16[3,448,112]{1,0,2:T(4,128)(2,1)}), bf16[3,448,448]{1,0,2:T(4,128)(2,1)}) %all-gather.3.cloned.1.call-update) | async-done | bytes 1204240 | tf_op jit(solution)/shard_map/all_gather | solution.py:38
  34.0 6.1 %fusion.88 = (bf16[1,448,448]{1,0,2:T(2,128)(2,1)S(1)}, bf16[1,448,448]{1,0,2:T(2,128)(2,1)S(1)}, bf16[1,448,448]{1,0,2:T(2,128)(2,1)}) fusion(bf16[3,448,448]{1,0,2:T(4,128)(2,1)} %all-gather.3.cloned.1.call-done), kind=kLoop, calls=%fused_computation.93 | loop fusion | bytes 2408448 | tf_op jit(solution)/shard_map/slice | solution.py:52
  40.1 17.2 %all-gather.5.cloned.1.call-done = bf16[3,448,448]{1,0,2:T(4,128)(2,1)} async-done(((bf16[3,448,112]{1,0,2:T(4,128)(2,1)}), bf16[3,448,448]{1,0,2:T(4,128)(2,1)}) %all-gather.5.cloned.1.call-update) | async-done | bytes 1204240 | tf_op jit(solution)/shard_map/all_gather | solution.py:56
  57.3 6.3 %fusion.87 = (bf16[1,448,448]{1,0,2:T(2,128)(2,1)}, bf16[1,448,448]{1,0,2:T(2,128)(2,1)}, bf16[1,448,448]{1,0,2:T(2,128)(2,1)}) fusion(bf16[3,448,448]{1,0,2:T(4,128)(2,1)} %all-gather.5.cloned.1.call-done), kind=kLoop, calls=%fused_computation.92 | loop fusion | bytes 2408448 | tf_op jit(solution)/shard_map/slice | solution.py:60
  63.6 2.4 copy.21
  66.0 2.0 copy.22
  68.0 1.9 copy.23
  69.9 3.5 %copy.24 = bf16[1,448,448]{2,1,0:T(8,128)(2,1)} copy(bf16[1,448,448]{1,0,2:T(2,128)(2,1)} %get-tuple-element.7) | data formatting | bytes 802816
  73.4 1.3 copy.25
  74.7 1.0 fusion.46
  75.7 3.1 %fusion.57 = f32[1024,448]{0,1:T(8,128)} fusion(bf16[1,448,448]{2,1,0:T(8,128)(2,1)S(1)} %copy.25, bf16[1,1024,448]{1,2,0:T(8,128)(2,1)} %param.5), kind=kOutput, calls=%fused_computation.71 | convolution fusion | flops 411041792 | bytes 3153920 | tf_op jit(solution)/shard_map/dot_general | solution.py:27
  78.8 1.9 fusion.74
  80.8 2.1 fusion.27
  82.8 0.0 copy-start.17
  82.8 2.3 fusion.40
  85.2 2.0 fusion.41
  87.2 0.2 pad_maximum_fusion.1
  87.4 1.8 copy.19
  89.2 2.5 %reshape.22 = bf16[448,1344]{1,0:T(8,128)(2,1)} reshape(bf16[448,3,448]{2,1,0:T(4,128)(2,1)S(1)} %bitcast.119) | data formatting | bytes 2408448
  91.7 0.0 reduce-scatter.9.cloned.1.call-update
  91.8 0.2 reduce-scatter.7.cloned.1.call-start
  92.0 3.2 %fusion.59 = f32[1024,448]{0,1:T(8,128)} fusion(bf16[1024,448]{0,1:T(8,128)(2,1)} %collective-permute-done.2, bf16[1,448,448]{2,1,0:T(8,128)(2,1)S(1)} %copy-done.10), kind=kOutput, calls=%fused_computation.73 | convolution fusion | flops 411041792 | bytes 3153920 | tf_op jit(solution)/shard_map/dot_general | solution.py:27
  95.2 1.3 copy.26
  96.5 4.2 %fusion.17 = bf16[1024,448]{0,1:T(8,128)(2,1)S(1)} fusion(bf16[1024,448]{0,1:T(8,128)(2,1)} %copy-done.17, f32[1024,448]{0,1:T(8,128)} %fusion.59, f32[1024,448]{0,1:T(8,128)S(1)} %copy-done.7, bf16[1024,448]{0,1:T(8,128)(2,1)} %collective-permute-done.2, bf16[1,448,448]{2,1,0:T(8,128)(2,1)S(1)} %copy.26, bf16[1,1024,448]{1,2,0:T(8,128)(2,1)} %param.5), kind=kOutput, calls=%fused_computation.27 | convolution fusion | flops 422051840 | bytes 7741440 | tf_op jit(solution)/shard_map/dot_general | solution.py:27
  100.7 4.5 %collective-permute-start.4 = (bf16[1024,448]{0,1:T(8,128)(2,1)S(1)}, bf16[1024,448]{0,1:T(8,128)(2,1)S(1)}, u32[]{:S(2)}, u32[]{:S(2)}) collective-permute-start(bf16[1024,448]{0,1:T(8,128)(2,1)S(1)} %fusion.17), channel_id=1, source_target_pairs={{0,8},{4,12},{1,9},{5,13},{2,10},{6,14},{3,11},{7,15},{16,24},{20,... | collective-permute-start | bytes 2752520 | tf_op jit(solution)/shard_map/ppermute | solution.py:12
  105.2 1.3 collective-permute-start.3
  106.5 0.8 fusion.43
  107.4 17.8 %collective-permute-done.4 = bf16[1024,448]{0,1:T(8,128)(2,1)S(1)} collective-permute-done((bf16[1024,448]{0,1:T(8,128)(2,1)S(1)}, bf16[1024,448]{0,1:T(8,128)(2,1)S(1)}, u32[]{:S(2)}, u32[]{:S(2)}) %collective-permute-start.4) | collective-permute-done | bytes 917536 | tf_op jit(solution)/shard_map/ppermute | solution.py:12
  125.2 0.8 fusion.42
  126.0 0.1 copy-done.18
  126.1 23.8 %collective-permute-done.3 = bf16[1024,448]{0,1:T(8,128)(2,1)S(1)} collective-permute-done((bf16[1024,448]{0,1:T(8,128)(2,1)S(1)}, bf16[1024,448]{0,1:T(8,128)(2,1)S(1)}, u32[]{:S(2)}, u32[]{:S(2)}) %collective-permute-start.3) | collective-permute-done | bytes 917536 | tf_op jit(solution)/shard_map/ppermute | solution.py:12
  149.9 0.9 copy-done.15
  150.8 0.8 fusion.44
  151.6 0.2 pad_maximum_fusion
  151.8 1.8 copy.17
  153.6 0.0 copy-start.9
  153.6 2.5 %reshape.20 = bf16[448,1344]{1,0:T(8,128)(2,1)} reshape(bf16[448,3,448]{2,1,0:T(4,128)(2,1)S(1)} %bitcast.120) | data formatting | bytes 2408448
  156.1 0.0 reduce-scatter.7.cloned.1.call-update
  156.2 0.0 copy-start.16
  156.2 0.6 fusion.69
  156.9 0.4 copy-done.1
  157.2 0.3 copy-done.16
  157.5 0.6 fusion.72
  158.2 0.5 copy-done.4
  158.7 0.1 copy-done.12
  158.8 0.5 copy-done.19
  159.3 2.7 %fusion.52 = bf16[1,1024,448]{1,2,0:T(8,128)(2,1)} fusion(f32[1024,448]{0,1:T(8,128)S(1)} %fusion.72, f32[1024,448]{0,1:T(8,128)S(1)} %fusion.69, bf16[1,1024,448]{1,2,0:T(8,128)(2,1)S(1)} %copy-done.4, bf16[1024,448]{0,1:T(8,128)(2,1)S(1)} %copy-done.14, bf16[1024,448]{0,1:T(8,128)(2,1)S(1)} %copy-done.19, bf16[1,448,448]{2,1,0:T(8,128)(2,1)S(1)} %copy-done.12), kind=kOutput, calls=%fused_computation.68 | convolution fusion | flops 422051840 | bytes 7741440 | tf_op jit(solution)/shard_map/dot_general | solution.py:27
  162.0 1.7 reshape.23
  163.7 0.3 copy.20
  164.0 15.7 %reduce-scatter.7.cloned.1.call-done = bf16[112,1344]{1,0:T(8,128)(2,1)} async-done(((bf16[448,1344]{1,0:T(8,128)(2,1)}), bf16[112,1344]{1,0:T(8,128)(2,1)}) %reduce-scatter.7.cloned.1.call-update) | async-done | bytes 301072
  179.8 1.7 reshape.21
  181.5 0.3 copy.18
  181.8 54.2 %all-reduce.2 = (f32[3,448,112]{2,1,0:T(8,128)}, f32[3,448,112]{2,1,0:T(8,128)}) all-reduce(bf16[3,448,112]{2,1,0:T(8,128)(2,1)S(1)} %copy.18, bf16[3,448,112]{2,1,0:T(8,128)(2,1)S(1)} %copy.20), channel_id=1, replica_groups=mesh['groups'=2,'seq'=4,'dp'=4] {'seq'}, use_global_device_ids=true, to_apply=%region_1.0 | all-reduce | flops 301056 | bytes 1806336 | tf_op jit(solution)/shard_map/psum | solution.py:82
  (34 shorter events, 0.1 us)
Async XLA Ops:
  7.2 4.5 %copy-start.2 = (bf16[1,1024,448]{1,2,0:T(8,128)(2,1)S(1)}, bf16[1,1024,448]{1,2,0:T(8,128)(2,1)}, u32[]{:S(2)}) copy-start(bf16[1,1024,448]{1,2,0:T(8,128)(2,1)} %param.4) | copy-start | bytes 2752516
  7.2 26.8 %all-gather.3.cloned.1.call-start = ((), (), s32[]{:S(2)}) async-start(), calls=%async_computation.2 | async-start | bytes 2293760 | tf_op jit(solution)/shard_map/all_gather | solution.py:38
  9.4 47.9 %all-gather.5.cloned.1.call-start = ((), (), s32[]{:S(2)}) async-start(), calls=%async_computation.3 | async-start | bytes 2293760 | tf_op jit(solution)/shard_map/all_gather | solution.py:56
  11.6 150.4 %reduce-scatter.9.cloned.1.call-start = ((), (), s32[]{:S(2)}) async-start(), calls=%async_computation.5 | async-start | bytes 1576960
  13.2 65.6 %collective-permute-start = (bf16[1024,448]{0,1:T(8,128)(2,1)}, bf16[1024,448]{0,1:T(8,128)(2,1)}, u32[]{:S(2)}, u32[]{:S(2)}) collective-permute-start(bf16[1024,448]{0,1:T(8,128)(2,1)} %fusion.26), channel_id=1, source_target_pairs={{0,8},{4,12},{1,9},{5,13},{2,10},{6,14},{3,11},{7,15},{16,24},{20,... | collective-permute-start | bytes 2752520 | tf_op jit(solution)/shard_map/ppermute | solution.py:12
  20.1 60.7 %collective-permute-start.1 = (bf16[1024,448]{0,1:T(8,128)(2,1)}, bf16[1024,448]{0,1:T(8,128)(2,1)}, u32[]{:S(2)}, u32[]{:S(2)}) collective-permute-start(bf16[1024,448]{0,1:T(8,128)(2,1)} %fusion.26), channel_id=1, source_target_pairs={{8,0},{12,4},{9,1},{13,5},{10,2},{14,6},{11,3},{15,7},{24,16},{28,... | collective-permute-start | bytes 2752520 | tf_op jit(solution)/shard_map/ppermute | solution.py:12
  21.4 63.8 %collective-permute-start.2 = (bf16[1024,448]{0,1:T(8,128)(2,1)}, bf16[1024,448]{0,1:T(8,128)(2,1)}, u32[]{:S(2)}, u32[]{:S(2)}) collective-permute-start(bf16[1024,448]{0,1:T(8,128)(2,1)} %bitcast), channel_id=1, source_target_pairs={} | collective-permute-start | bytes 2752520 | tf_op jit(solution)/shard_map/ppermute | solution.py:12
  66.0 12.8 %copy-start = (bf16[1,448,448]{2,1,0:T(8,128)(2,1)}, bf16[1,448,448]{2,1,0:T(8,128)(2,1)S(1)}, u32[]{:S(2)}) copy-start(bf16[1,448,448]{2,1,0:T(8,128)(2,1)S(1)} %copy.21) | copy-start | bytes 1204228
  68.0 5.4 %copy-start.6 = (bf16[1,448,448]{1,0,2:T(2,128)(2,1)S(1)}, bf16[1,448,448]{1,0,2:T(2,128)(2,1)}, u32[]{:S(2)}) copy-start(bf16[1,448,448]{1,0,2:T(2,128)(2,1)} %get-tuple-element.6) | copy-start | bytes 1204228
  69.9 4.8 %copy-start.8 = (bf16[1,448,448]{2,1,0:T(8,128)(2,1)S(1)}, bf16[1,448,448]{2,1,0:T(8,128)(2,1)}, u32[]{:S(2)}) copy-start(bf16[1,448,448]{2,1,0:T(8,128)(2,1)} %copy.22) | copy-start | bytes 1204228
  78.8 1.9 copy-start.11
  82.8 2.4 copy-start.17
  89.2 2.8 %copy-start.10 = (bf16[1,448,448]{2,1,0:T(8,128)(2,1)S(1)}, bf16[1,448,448]{2,1,0:T(8,128)(2,1)}, u32[]{:S(2)}) copy-start(bf16[1,448,448]{2,1,0:T(8,128)(2,1)} %copy.24) | copy-start | bytes 1204228
  91.7 3.4 %copy-start.5 = (bf16[1,448,448]{1,0,2:T(2,128)(2,1)S(1)}, bf16[1,448,448]{1,0,2:T(2,128)(2,1)}, u32[]{:S(2)}) copy-start(bf16[1,448,448]{1,0,2:T(2,128)(2,1)} %get-tuple-element.5) | copy-start | bytes 1204228
  91.7 4.8 %copy-start.7 = (f32[1024,448]{0,1:T(8,128)S(1)}, f32[1024,448]{0,1:T(8,128)}, u32[]{:S(2)}) copy-start(f32[1024,448]{0,1:T(8,128)} %fusion.57) | copy-start | bytes 5505028
  91.8 88.0 %reduce-scatter.7.cloned.1.call-start = ((), (), s32[]{:S(2)}) async-start(), calls=%async_computation.4 | async-start | bytes 1576960
  96.5 10.0 %copy-start.3 = (bf16[1,1024,448]{1,2,0:T(8,128)(2,1)S(1)}, bf16[1,1024,448]{1,2,0:T(8,128)(2,1)}, u32[]{:S(2)}) copy-start(bf16[1,1024,448]{1,2,0:T(8,128)(2,1)} %param.4) | copy-start | bytes 2752516
  100.7 6.7 %copy-start.13 = (bf16[1024,448]{0,1:T(8,128)(2,1)}, bf16[1024,448]{0,1:T(8,128)(2,1)S(1)}, u32[]{:S(2)}) copy-start(bf16[1024,448]{0,1:T(8,128)(2,1)S(1)} %fusion.17) | copy-start | bytes 2752516
  100.7 24.5 %collective-permute-start.4 = (bf16[1024,448]{0,1:T(8,128)(2,1)S(1)}, bf16[1024,448]{0,1:T(8,128)(2,1)S(1)}, u32[]{:S(2)}, u32[]{:S(2)}) collective-permute-start(bf16[1024,448]{0,1:T(8,128)(2,1)S(1)} %fusion.17), channel_id=1, source_target_pairs={{0,8},{4,12},{1,9},{5,13},{2,10},{6,14},{3,11},{7,15},{16,24},{20,... | collective-permute-start | bytes 2752520 | tf_op jit(solution)/shard_map/ppermute | solution.py:12
  105.2 44.7 %collective-permute-start.3 = (bf16[1024,448]{0,1:T(8,128)(2,1)S(1)}, bf16[1024,448]{0,1:T(8,128)(2,1)S(1)}, u32[]{:S(2)}, u32[]{:S(2)}) collective-permute-start(bf16[1024,448]{0,1:T(8,128)(2,1)S(1)} %fusion.17), channel_id=1, source_target_pairs={{8,0},{12,4},{9,1},{13,5},{10,2},{14,6},{11,3},{15,7},{24,16},{28,... | collective-permute-start | bytes 2752520 | tf_op jit(solution)/shard_map/ppermute | solution.py:12
  125.2 0.9 copy-start.18
  149.9 0.9 copy-start.15
  153.6 2.5 %copy-start.9 = (bf16[1,448,448]{2,1,0:T(8,128)(2,1)S(1)}, bf16[1,448,448]{2,1,0:T(8,128)(2,1)}, u32[]{:S(2)}) copy-start(bf16[1,448,448]{2,1,0:T(8,128)(2,1)} %copy.22) | copy-start | bytes 1204228
  153.6 2.5 %copy-start.14 = (bf16[1024,448]{0,1:T(8,128)(2,1)S(1)}, bf16[1024,448]{0,1:T(8,128)(2,1)}, u32[]{:S(2)}) copy-start(bf16[1024,448]{0,1:T(8,128)(2,1)} %copy-done.13) | copy-start | bytes 2752516
  156.2 1.0 copy-start.1
  156.2 1.3 copy-start.16
  157.5 1.2 copy-start.4
  157.5 1.3 copy-start.12
  157.5 1.8 copy-start.19
Sparse Core Ops, SparseCore 0:
  10.1 23.8 all-gather.2
  36.1 21.1 all-gather.4
  91.9 26.2 reduce-scatter.8
  156.3 23.4 reduce-scatter.6
where the time goes:
time: 243 us
  waiting for transfers between devices  85.6 us (35%)
  blocking collectives  54.2 us (22%)
  local copies, waits for them, and re-layouts  44.6 us (18%)
  matrix products  26.1 us (11%)
  starting transfers between devices  15.9 us (7%)
  between operations  14.1 us (6%)
    psum x1, blocking collectives, on_device(): lax.psum(lax.psum_scatter(part_one, 'dp', scatter_dimension=2, tiled=True...  54.2 us
    ppermute x5, waiting for transfers between devices, shifted(): return lax.ppermute(block, axis, route)  41.6 us
    unnamed x56, local copies, waits for them, and re-layouts  32.2 us
    all_gather x1, waiting for transfers between devices, on_device(): full_two = lax.all_gather(weight_two, 'dp', axis=2, tiled=True)  17.2 us
    unnamed x6, waiting for transfers between devices  15.8 us
    ppermute x5, starting transfers between devices, shifted(): return lax.ppermute(block, axis, route)  15.6 us
    dot_general x6, matrix products, back_product(): lax.dot_general(tap, weight, (((1,), (1,)), ((), ())), preferred_element_...  14.4 us
    all_gather x1, waiting for transfers between devices, on_device(): full_one = lax.all_gather(first_weight_matrix, 'dp', axis=2, tiled=True)  11 us
  transfers between devices with their start and end apart: 9, of which 5 were waited for; matrix products, arithmetic and copies ran while one was open for 24% of the time, Pallas kernels for 0%

commit v1 on v0

--- a/solution.py
+++ b/solution.py
@@ -1,9 +1,295 @@
+import functools
 import math
 
 import jax
 import jax.numpy as jnp
 from jax import lax
+from jax.experimental import pallas as pl
+from jax.experimental.pallas import tpu as pltpu
 from jax.sharding import PartitionSpec as P
+
+FIRST_SHIFT = 2
+SECOND_SHIFT = 4
+CHUNKS = (2, 2)
+F32 = jnp.float32
+BF16 = jnp.bfloat16
+
+
+def gelu_pair(x):
+    s = math.sqrt(2.0 / math.pi)
+    square = x * x
+    half = 0.5 + 0.5 * jnp.tanh(x * (s + (0.044715 * s) * square))
+    bend = x * (2.0 * s + (6.0 * 0.044715 * s) * square)
+    return x * half, half * (1.0 + (1.0 - half) * bend)
+
+
+def dot_nn(a, b):
+    return lax.dot_general(a, b, (((1,), (0,)), ((), ())), preferred_element_type=F32)
+
+
+def dot_nt(a, b):
+    return lax.dot_general(a, b, (((1,), (1,)), ((), ())), preferred_element_type=F32)
+
+
+def dot_tn(a, b):
+    return lax.dot_general(a, b, (((0,), (0,)), ((), ())), preferred_element_type=F32)
+
+
+VMEM = pl.BlockSpec(memory_space=pltpu.VMEM)
+SMEM = pl.BlockSpec(memory_space=pltpu.SMEM)
+ANY = pl.BlockSpec(memory_space=pl.ANY)
+HBM = pl.BlockSpec(memory_space=pltpu.HBM)
+
+
+def call(body, name, out, operands, specs, out_specs=None, scratch=(), aliases=None, limit=8):
+    return pl.pallas_call(
+        body,
+        out_shape=[jax.ShapeDtypeStruct(*o) for o in out],
+        in_specs=specs,
+        out_specs=out_specs or [VMEM] * len(out),
+        scratch_shapes=scratch,
+        input_output_aliases=aliases or {},
+        compiler_params=pltpu.CompilerParams(vmem_limit_bytes=limit << 20),
+        name=name,
+    )(*operands)
+
+
+def lanes(start, size):
+    return pl.ds(pl.multiple_of(start, 128), size)
+
+
+def pack_kernel(where, x_ref, c_ref, *refs):
+    wires, sems = refs[:-1], refs[-1]
+    copies, start = [], 0
+    for c, wire in enumerate(wires):
+        size = wire.shape[2]
+        for j, ref in enumerate((x_ref, c_ref)):
+            source = ref.at[:, lanes(where[4] + start, size)]
+            copies.append(pltpu.make_async_copy(source, wire.at[j], sems.at[2 * c + j]))
+        start += size
+    for copy in copies:
+        copy.start()
+    for copy in copies:
+        copy.wait()
+
+
+def turn_kernel(w_ref, w2_ref, after_ref, out_ref, taps, sems):
+    del after_ref
+    copies = [
+        pltpu.make_async_copy(w_ref, taps.at[pl.ds(0, 3)], sems.at[0]),
+        pltpu.make_async_copy(w2_ref.at[1], taps.at[3], sems.at[1]),
+    ]
+    for copy in copies:
+        copy.start()
+    for copy in copies:
+        copy.wait()
+    for k in range(4):
+        out_ref[k] = taps[k].T
+
+
+def join_kernel(where, *refs):
+    pieces, (out_ref, across_ref) = refs[:-2], refs[-2:]
+    shard = pieces[0].shape[1]
+    for m, ref in enumerate(pieces):
+        rows = pl.ds(pl.multiple_of(lax.bitwise_xor(where[3], m) * shard, 16), shard)
+        for k in range(4):
+            out_ref[k, rows, :] = ref[k]
+    for k in range(4):
+        across_ref[k] = out_ref[k].T
+
+
+def both(o_ref, where, start, size, wire):
+    return jnp.concatenate([o_ref[:, lanes(where[0] + start, size)], wire], axis=1)
+
+
+def ahead_kernel(start, first, last, factor, where, x_ref, c_ref, wire_ref, w_ref, across_ref, *refs):
+    if not first:
+        sums_in, refs = refs[0], refs[1:]
+    mid_ref, refs = refs[0], refs[1:]
+    size = wire_ref.shape[2]
+    q = where[1]
+    r = 2 - q
+    x = both(x_ref, where, start, size, wire_ref[0]).astype(F32)
+    cot = both(c_ref, where, start, size, wire_ref[1])
+    act = gelu_pair(x)[0].astype(BF16)
+    act_o, act_p = act[:, :size], act[:, size:]
+    cross = jnp.concatenate([dot_nn(w_ref[q], act_p), dot_nn(w_ref[r], act_o)], axis=1)
+    hidden = (x + dot_nn(w_ref[1], act) + cross).astype(BF16).astype(F32)
+    act_one, slope_one = gelu_pair(hidden)
+    mid = (cot.astype(F32) + slope_one * dot_nn(across_ref[3], cot)).astype(BF16)
+    mid_ref[...] = mid
+    mid_o, mid_p = mid[:, :size], mid[:, size:]
+    terms = (
+        (3, cot, act_one.astype(BF16)),
+        (1, mid, act),
+        (q, mid_o, act_p),
+        (r, mid_p, act_o),
+    )
+    if not last:
+        (sums,) = refs
+        for k, left, right in terms:
+            value = dot_nt(left, right)
+            sums[k] = value if first else sums_in[k] + value
+        return
+    keep_ref, give_ref, total = refs
+    for k, left, right in terms:
+        total[k] = ((sums_in[k] + dot_nt(left, right)) * factor).astype(BF16)
+    shard = keep_ref.shape[2]
+    for ref, core in ((keep_ref, where[2]), (give_ref, 1 - where[2])):
+        for j in range(2):
+            side = lax.bitwise_xor(where[6], 1 - j)
+            rows = pl.ds(pl.multiple_of((2 * side + core) * shard, 16), shard)
+            for k in range(2):
+                level = lax.bitwise_xor(where[5], 1 - k)
+                pair = [total[level, rows, :], total[level + 2, rows, :]]
+                ref[j, k] = jnp.concatenate(pair, axis=1)
+
+
+def back_kernel(start, where, x_ref, wire_ref, mid_ref, across_ref, own_ref, give_ref):
+    size = wire_ref.shape[2]
+    q = where[1]
+    r = 2 - q
+    slope = gelu_pair(both(x_ref, where, start, size, wire_ref[0]).astype(F32))[1]
+    mid = mid_ref[...]
+    mid_o, mid_p = mid[:, :size], mid[:, size:]
+    cross = jnp.concatenate([dot_nn(across_ref[r], mid_p), dot_nn(across_ref[q], mid_o)], axis=1)
+    delta = dot_nn(across_ref[1], mid) + cross
+    grad = (mid.astype(F32) + slope * delta).astype(BF16)
+    own_ref[...] = grad[:, :size]
+    give_ref[...] = grad[:, size:]
+
+
+def finish_kernel(where, mine_ref, theirs_ref, one_ref, two_ref):
+    chans = one_ref.shape[1]
+    even = where[5] == 0
+    mine, theirs = mine_ref[...], theirs_ref[...]
+    for want, taps in ((even, ((one_ref, 0), (one_ref, 2))), (~even, ((one_ref, 1), (two_ref, 1)))):
+        terms = jnp.where(want, mine, theirs).astype(F32)
+        for j, (out, k) in enumerate(taps):
+            out[k] = terms[:, j * chans : (j + 1) * chans].T
+    two_ref[0] = jnp.zeros(two_ref.shape[1:], F32)
+    two_ref[2] = jnp.zeros(two_ref.shape[1:], F32)
+
+
+def place_kernel(where, *refs):
+    out_ref, refs = refs[-1], refs[:-2]
+    count = len(CHUNKS)
+    for base, pieces in ((where[0], refs[:count]), (where[4], refs[count:])):
+        start = 0
+        for ref in pieces:
+            out_ref[:, lanes(base + start, ref.shape[1])] = ref[...]
+            start += ref.shape[1]
+
+
+def swapped(value, axis, bit):
+    route = [(i, i ^ bit) for i in range(lax.axis_size(axis))]
+    return lax.ppermute(value, axis, route)
+
+
+def added(a, b):
+    return (a.astype(F32) + b.astype(F32)).astype(BF16)
+
+
+def on_pairs(inputs, cotangent, first_weight_matrix, weight_two):
+    chans = inputs.shape[2]
+    block = inputs.shape[1]
+    shard = chans // 4
+    half = block // 2
+    sizes = [half * part // sum(CHUNKS) for part in CHUNKS]
+    factor = 1.0 / math.sqrt(
+        inputs.shape[0] * lax.axis_size("dp") * inputs.shape[1] * lax.axis_size("seq")
+    )
+    seq, dp = lax.axis_index("seq"), lax.axis_index("dp")
+    low = seq < FIRST_SHIFT
+    keep_at = jnp.where(low, 0, half)
+    level, side, core = seq % 2, dp // 2, dp % 2
+    where = jnp.stack([keep_at, jnp.where(low, 2, 0), core, dp, half - keep_at, level, side])
+    where = where.astype(jnp.int32)
+    x, cot = inputs.reshape(block, chans).T, cotangent.reshape(block, chans).T
+
+    packed = call(
+        pack_kernel,
+        "pack",
+        [((2, chans, size), BF16) for size in sizes],
+        [where, x, cot],
+        [SMEM, HBM, HBM],
+        scratch=[pltpu.SemaphoreType.DMA((2 * len(sizes),))],
+    )
+    wires = [swapped(wire, "seq", FIRST_SHIFT) for wire in packed]
+    (own_shard,) = call(
+        turn_kernel,
+        "turn",
+        [((4, shard, chans), BF16)],
+        [first_weight_matrix, weight_two, packed[-1]],
+        [HBM, HBM, ANY],
+        scratch=[pltpu.VMEM((4, chans, shard), BF16), pltpu.SemaphoreType.DMA((2,))],
+    )
+    shards = [own_shard] + [swapped(own_shard, "dp", m) for m in (1, 2, 3)]
+    w, across = call(
+        join_kernel,
+        "join",
+        [((4, chans, chans), BF16)] * 2,
+        [where, *shards],
+        [SMEM] + [VMEM] * 4,
+    )
+
+    start, sums, own, back = 0, [], [], []
+    for c, size in enumerate(sizes):
+        last = c == len(sizes) - 1
+        out = [((chans, 2 * size), BF16)]
+        out += [((2, 2, shard, 2 * chans), BF16)] * 2 if last else [((4, chans, chans), F32)]
+        operands = [where, x, cot, wires[c], w, across] + sums
+        mid, *rest = call(
+            functools.partial(ahead_kernel, start, c == 0, last, factor),
+            f"ahead_{c}",
+            out,
+            operands,
+            [SMEM] + [VMEM] * (len(operands) - 1),
+            scratch=[pltpu.VMEM((4, chans, chans), BF16)] if last else [],
+            aliases={6: 1} if sums and not last else {},
+        )
+        if last:
+            keep, give = rest
+        else:
+            sums = rest
+        mine, theirs = call(
+            functools.partial(back_kernel, start),
+            f"back_{c}",
+            [((chans, size), BF16)] * 2,
+            [where, x, wires[c], mid, across],
+            [SMEM] + [VMEM] * 4,
+        )
+        own.append(mine)
+        back.append(theirs)
+        start += size
+
+    back[0], give = lax.optimization_barrier((back[0], give))
+    whole = jnp.concatenate(back, axis=1)
+    returned = [swapped(part, "seq", FIRST_SHIFT) for part in (whole[:, :128], whole[:, 128:])]
+    got_core = swapped(give, "dp", 1)
+    theirs = swapped(added(keep[0], got_core[0]), "dp", 2)
+    mine = added(keep[1], got_core[1])
+    theirs, returned[0] = lax.optimization_barrier((theirs, returned[0]))
+    theirs, mine = added(mine[0], theirs[0]), added(mine[1], theirs[1])
+    theirs, returned[1] = lax.optimization_barrier((swapped(theirs, "seq", 1), returned[1]))
+    mine = added(mine, theirs)
+    mine = added(mine, swapped(mine, "seq", 2))
+    theirs = swapped(mine, "seq", 1)
+    (input_grad,) = call(
+        place_kernel,
+        "place",
+        [((chans, block), BF16)],
+        [where, *own, *returned, mine],
+        [SMEM] + [VMEM] * (len(own) + len(returned)) + [ANY],
+    )
+    grad_one, grad_two = call(
+        finish_kernel,
+        "finish",
+        [((3, chans, shard), F32)] * 2,
+        [where, mine, theirs],
+        [SMEM, VMEM, VMEM],
+    )
+    return (input_grad.T.reshape(inputs.shape), grad_one, grad_two)
 
 
 def shifted(block, axis, distance):
@@ -29,7 +315,7 @@
     )
 
 
-def on_device(inputs, cotangent, first_weight_matrix, weight_two):
+def on_shifts(inputs, cotangent, first_weight_matrix, weight_two):
     chans = inputs.shape[2]
     rows = inputs.shape[0] * inputs.shape[1]
     factor = 1.0 / math.sqrt(
@@ -85,6 +371,19 @@
     return (input_grad.reshape(inputs.shape), grad_one, grad_two)
 
 
+def on_device(inputs, *others):
+    seq, dp = lax.axis_size("seq"), lax.axis_size("dp")
+    if (
+        seq == 2 * FIRST_SHIFT
+        and seq <= SECOND_SHIFT
+        and dp == 4
+        and inputs.shape[0] == 1
+        and inputs.shape[1] % (256 * sum(CHUNKS)) == 0
+    ):
+        return on_pairs(inputs, *others)
+    return on_shifts(inputs, *others)
+
+
 def solution(mesh):
     placed = (
         P(("groups", "dp"), "seq", None),

time: 243 us -> 97.5 us (0.40)
  blocking collectives: 54.2 us -> 0 us
  local copies, waits for them, and re-layouts: 44.6 us -> 2.47 us
  matrix products: 26.1 us -> 0 us
  waiting for transfers between devices: 85.6 us -> 67.5 us
  Pallas kernels: 0 us -> 14.4 us
  between operations: 14.1 us -> 0.79 us
  starting transfers between devices: 15.9 us -> 11.7 us
    psum x1 -> x0, blocking collectives: 54.2 us -> none  [on_device(): lax.psum(lax.psum_scatter(part_one, 'dp', scatter_dimension=2, tiled=True...]
    unnamed x56 -> x12, local copies, waits for them, and re-layouts: 32.2 us -> 2.38 us
    all_gather x2 -> x0, waiting for transfers between devices: 28.2 us -> none  [the longest x1 17.2 us: on_device(): full_two = lax.all_gather(weight_two, 'dp', axis=2, tiled=True)]
    dot_general x14 -> x0, matrix products: 26.1 us -> none  [the longest x6 14.4 us: back_product(): lax.dot_general(tap, weight, (((1,), (1,)), ((), ())), preferred_element_...]
    ppermute x5 -> x12, waiting for transfers between devices: 41.6 us -> 67.5 us  [swapped(): return lax.ppermute(value, axis, route)]
    unnamed x6 -> x0, waiting for transfers between devices: 15.8 us -> none
    pallas_call x0 -> x9, Pallas kernels: none -> 14.4 us  [call(): pl.pallas_call(body, out_shape=[jax.ShapeDtypeStruct(*o) for o in out], i...]
    slice x2 -> x1, local copies, waits for them, and re-layouts: 12.4 us -> 0.01 us  [on_pairs(): whole[:, :128]]
  transfers between devices with their start and end apart: 9 -> 12, of which waited for: 5 -> 10; matrix products, arithmetic and copies ran while one was open for 24% -> 0% of each run, Pallas kernels for 0% -> 9%
where the time goes in v1:
time: 97.5 us; the launch traced here: 97.3 us
  waiting for transfers between devices  67.5 us (69%)
  Pallas kernels  14.4 us (15%)
  starting transfers between devices  11.7 us (12%)
  local copies, waits for them, and re-layouts  2.47 us (3%)
    ppermute x12, waiting for transfers between devices, swapped(): return lax.ppermute(value, axis, route)  67.5 us
    pallas_call x9, Pallas kernels, call(): pl.pallas_call(body, out_shape=[jax.ShapeDtypeStruct(*o) for o in out], i...  14.4 us
    ppermute x12, starting transfers between devices, swapped(): return lax.ppermute(value, axis, route)  11.7 us
    unnamed x12, local copies, waits for them, and re-layouts  2.38 us
  transfers between devices with their start and end apart: 12, of which 10 were waited for; matrix products, arithmetic and copies ran while one was open for 0% of the time, Pallas kernels for 9%

profile of v1, /device:TPU:0, one launch (start us, length us, event | category | flops | bytes accessed | tf_op | source)
XLA Modules:
  0.0 97.3 jit_solution(2065425547473068803)
XLA Ops:
  0.7 0.1 stack.31.where
  0.7 0.0 copy-start
  0.8 1.2 %copy-done = bf16[1,1024,448]{1,2,0:T(8,128)(2,1)S(1)} copy-done((bf16[1,1024,448]{1,2,0:T(8,128)(2,1)S(1)}, bf16[1,1024,448]{1,2,0:T(8,128)(2,1)}, u32[]{:S(2)}) %copy-start) | copy-done | bytes 917528
  1.9 0.0 copy-start.2
  1.9 1.2 %copy-done.2 = bf16[1,1024,448]{1,2,0:T(8,128)(2,1)S(1)} copy-done((bf16[1,1024,448]{1,2,0:T(8,128)(2,1)S(1)}, bf16[1,1024,448]{1,2,0:T(8,128)(2,1)}, u32[]{:S(2)}) %copy-start.2) | copy-done | bytes 917528
  3.1 0.0 copy-start.4
  3.1 0.0 copy-start.5
  3.1 0.7 pack.1
  3.8 0.0 copy-start.1
  3.8 0.0 copy-start.3
  3.9 4.1 %collective-permute-start = (bf16[2,448,256]{2,1,0:T(8,128)(2,1)S(1)}, bf16[2,448,256]{2,1,0:T(8,128)(2,1)S(1)}, u32[]{:S(2)}, u32[]{:S(2)}) collective-permute-start(bf16[2,448,256]{2,1,0:T(8,128)(2,1)S(1)} %get-tuple-element.24), channel_id=1, source_target_pairs={{0,8},{4,12},{8,0},{12,4},{1,9},{5,13},{9,1},{13,5},{2,10},{6,14},... | collective-permute-start | bytes 1376264 | tf_op jit(solution)/shard_map/ppermute | solution.py:186
  8.0 0.1 collective-permute-start.4
  8.0 0.0 copy-done.4
  8.0 0.0 copy-done.5
  8.0 0.5 turn.1.refs_0_
  8.5 0.7 collective-permute-start.3
  9.2 1.2 %collective-permute-start.2 = (bf16[4,112,448]{2,1,0:T(8,128)(2,1)S(1)}, bf16[4,112,448]{2,1,0:T(8,128)(2,1)S(1)}, u32[]{:S(2)}, u32[]{:S(2)}) collective-permute-start(bf16[4,112,448]{2,1,0:T(8,128)(2,1)S(1)} %turn.1.refs_0_), channel_id=1, source_target_pairs={{0,2},{1,3},{2,0},{3,1},{4,6},{5,7},{6,4},{7,5},{8,10},{9,11},{10,... | collective-permute-start | bytes 1204232 | tf_op jit(solution)/shard_map/ppermute | solution.py:186
  10.4 0.1 collective-permute-start.1
  10.5 10.6 %collective-permute-done.3.refs_3_ = bf16[4,112,448]{2,1,0:T(8,128)(2,1)S(1)} collective-permute-done((bf16[4,112,448]{2,1,0:T(8,128)(2,1)S(1)}, bf16[4,112,448]{2,1,0:T(8,128)(2,1)S(1)}, u32[]{:S(2)}, u32[]{:S(2)}) %collective-permute-start.3) | collective-permute-done | bytes 401440 | tf_op jit(solution)/shard_map/ppermute | solution.py:186
  21.1 10.1 %collective-permute-done.2.refs_2_ = bf16[4,112,448]{2,1,0:T(8,128)(2,1)S(1)} collective-permute-done((bf16[4,112,448]{2,1,0:T(8,128)(2,1)S(1)}, bf16[4,112,448]{2,1,0:T(8,128)(2,1)S(1)}, u32[]{:S(2)}, u32[]{:S(2)}) %collective-permute-start.2) | collective-permute-done | bytes 401440 | tf_op jit(solution)/shard_map/ppermute | solution.py:186
  31.2 0.0 collective-permute-done.1.refs_1_
  31.2 1.2 %join.1 = (bf16[4,448,448]{2,1,0:T(8,128)(2,1)S(1)}, bf16[4,448,448]{2,1,0:T(8,128)(2,1)S(1)}) custom-call(s32[7]{0:T(128)S(1)} %stack.31.where, bf16[4,112,448]{2,1,0:T(8,128)(2,1)S(1)} %turn.1.refs_0_, bf16[4,112,448]{2,1,0:T(8,128)(2,1)S(1)} %collective-permute-done.1.refs_1_, bf16[4,112,448]{2,1,0:T(8,128)(2,1)S(1)} %collective-permute-done.2.refs_2_, ...), custom_call_target="tpu_custom_call" | custom-call | tf_op jit(solution)/shard_map/join/pallas_call | solution.py:45
  32.5 6.5 %collective-permute-done.wire_ref = bf16[2,448,256]{2,1,0:T(8,128)(2,1)S(1)} collective-permute-done((bf16[2,448,256]{2,1,0:T(8,128)(2,1)S(1)}, bf16[2,448,256]{2,1,0:T(8,128)(2,1)S(1)}, u32[]{:S(2)}, u32[]{:S(2)}) %collective-permute-start) | collective-permute-done | bytes 458784 | tf_op jit(solution)/shard_map/ppermute | solution.py:186
  39.0 0.0 copy-done.1
  39.0 0.0 copy-done.3
  39.0 2.5 %ahead_0.1 = (bf16[448,512]{1,0:T(8,128)(2,1)S(1)}, f32[4,448,448]{2,1,0:T(8,128)S(1)}) custom-call(s32[7]{0:T(128)S(1)} %stack.31.where, bf16[448,1024]{1,0:T(8,128)(2,1)S(1)} %bitcast.36, bf16[448,1024]{1,0:T(8,128)(2,1)S(1)} %bitcast.41, bf16[2,448,256]{2,1,0:T(8,128)(2,1)S(1)} %collective-permute-done.wire_ref, ...), custom_call_target="tpu_custom_call" | custom-call | tf_op jit(solution)/shard_map/ahead_0/pallas_call | solution.py:45
  41.5 1.5 %back_0.1 = (bf16[448,256]{1,0:T(8,128)(2,1)S(1)}, bf16[448,256]{1,0:T(8,128)(2,1)S(1)}) custom-call(s32[7]{0:T(128)S(1)} %stack.31.where, bf16[448,1024]{1,0:T(8,128)(2,1)S(1)} %bitcast.37, bf16[2,448,256]{2,1,0:T(8,128)(2,1)S(1)} %collective-permute-done.wire_ref, bf16[448,512]{1,0:T(8,128)(2,1)S(1)} %get-tuple-element.28.mid_ref, ...), custom_call_target="tpu_custom_call" | custom-call | tf_op jit(solution)/shard_map/back_0/pallas_call | solution.py:45
  43.1 4.9 %collective-permute-done.4.wire_ref = bf16[2,448,256]{2,1,0:T(8,128)(2,1)S(1)} collective-permute-done((bf16[2,448,256]{2,1,0:T(8,128)(2,1)S(1)}, bf16[2,448,256]{2,1,0:T(8,128)(2,1)S(1)}, u32[]{:S(2)}, u32[]{:S(2)}) %collective-permute-start.4) | collective-permute-done | bytes 458784 | tf_op jit(solution)/shard_map/ppermute | solution.py:186
  48.0 2.8 %ahead_1.1 = (bf16[448,512]{1,0:T(8,128)(2,1)S(1)}, bf16[2,2,112,896]{3,2,1,0:T(8,128)(2,1)S(1)}, bf16[2,2,112,896]{3,2,1,0:T(8,128)(2,1)S(1)}) custom-call(s32[7]{0:T(128)S(1)} %stack.31.where, bf16[448,1024]{1,0:T(8,128)(2,1)S(1)} %bitcast.38, bf16[448,1024]{1,0:T(8,128)(2,1)S(1)} %bitcast.42, bf16[2,448,256]{2,1,0:T(8,128)(2,1)S(1)} %collective-permute-done.4.wire_ref, ...), custom_call_target="tpu_custom_call" | custom-call | tf_op jit(solution)/shard_map/ahead_1/pallas_call | solution.py:45
  50.8 0.1 collective-permute-start.5
  50.9 2.3 %collective-permute-done.5 = bf16[2,2,112,896]{3,2,1,0:T(8,128)(2,1)S(1)} collective-permute-done((bf16[2,2,112,896]{3,2,1,0:T(8,128)(2,1)S(1)}, bf16[2,2,112,896]{3,2,1,0:T(8,128)(2,1)S(1)}, u32[]{:S(2)}, u32[]{:S(2)}) %collective-permute-start.5) | collective-permute-done | bytes 802848 | tf_op jit(solution)/shard_map/ppermute | solution.py:186
  53.2 0.2 add_convert_fusion
  53.4 1.6 %collective-permute-start.6 = (bf16[2,112,896]{2,1,0:T(8,128)(2,1)S(1)}, bf16[2,112,896]{2,1,0:T(8,128)(2,1)S(1)}, u32[]{:S(2)}, u32[]{:S(2)}) collective-permute-start(bf16[2,112,896]{2,1,0:T(8,128)(2,1)S(1)} %get-tuple-element.46), channel_id=1, source_target_pairs={{0,2},{1,3},{2,0},{3,1},{4,6},{5,7},{6,4},{7,5},{8,10},{9,11},{10,... | collective-permute-start | bytes 1204232 | tf_op jit(solution)/shard_map/ppermute | solution.py:186
  55.0 0.1 collective-permute-start.7
  55.1 1.6 %back_1.1 = (bf16[448,256]{1,0:T(8,128)(2,1)S(1)}, bf16[448,256]{1,0:T(8,128)(2,1)S(1)}) custom-call(s32[7]{0:T(128)S(1)} %stack.31.where, bf16[448,1024]{1,0:T(8,128)(2,1)S(1)} %bitcast.39, bf16[2,448,256]{2,1,0:T(8,128)(2,1)S(1)} %collective-permute-done.4.wire_ref, bf16[448,512]{1,0:T(8,128)(2,1)S(1)} %get-tuple-element.31.mid_ref, ...), custom_call_target="tpu_custom_call" | custom-call | tf_op jit(solution)/shard_map/back_1/pallas_call | solution.py:45
  56.7 3.0 %collective-permute-start.9 = (bf16[448,384]{1,0:T(8,128)(2,1)S(1)}, bf16[448,384]{1,0:T(8,128)(2,1)S(1)}, u32[]{:S(2)}, u32[]{:S(2)}) collective-permute-start(bf16[448,384]{1,0:T(8,128)(2,1)S(1)} %pad_maximum_fusion), channel_id=1, source_target_pairs={{0,8},{4,12},{8,0},{12,4},{1,9},{5,13},{9,1},{13,5},{2,10},{6,14},... | collective-permute-start | bytes 1032200 | tf_op jit(solution)/shard_map/ppermute | solution.py:186
  59.7 11.5 %collective-permute-done.7.refs_2_ = bf16[448,128]{1,0:T(8,128)(2,1)S(1)} collective-permute-done((bf16[448,128]{1,0:T(8,128)(2,1)S(1)}, bf16[448,128]{1,0:T(8,128)(2,1)S(1)}, u32[]{:S(2)}, u32[]{:S(2)}) %collective-permute-start.7) | collective-permute-done | bytes 114720 | tf_op jit(solution)/shard_map/ppermute | solution.py:186
  71.2 0.0 collective-permute-done.6
  71.3 0.1 collective-permute-start.8
  71.4 6.9 %collective-permute-done.9.refs_3_ = bf16[448,384]{1,0:T(8,128)(2,1)S(1)} collective-permute-done((bf16[448,384]{1,0:T(8,128)(2,1)S(1)}, bf16[448,384]{1,0:T(8,128)(2,1)S(1)}, u32[]{:S(2)}, u32[]{:S(2)}) %collective-permute-start.9) | collective-permute-done | bytes 344096 | tf_op jit(solution)/shard_map/ppermute | solution.py:186
  78.2 2.0 %collective-permute-done.8 = bf16[112,896]{1,0:T(8,128)(2,1)S(1)} collective-permute-done((bf16[112,896]{1,0:T(8,128)(2,1)S(1)}, bf16[112,896]{1,0:T(8,128)(2,1)S(1)}, u32[]{:S(2)}, u32[]{:S(2)}) %collective-permute-start.8) | collective-permute-done | bytes 200736 | tf_op jit(solution)/shard_map/ppermute | solution.py:186
  80.3 0.1 fusion.1
  80.3 0.4 collective-permute-start.10
  80.8 8.8 %collective-permute-done.10 = bf16[112,896]{1,0:T(8,128)(2,1)S(1)} collective-permute-done((bf16[112,896]{1,0:T(8,128)(2,1)S(1)}, bf16[112,896]{1,0:T(8,128)(2,1)S(1)}, u32[]{:S(2)}, u32[]{:S(2)}) %collective-permute-start.10) | collective-permute-done | bytes 200736 | tf_op jit(solution)/shard_map/ppermute | solution.py:186
  89.5 0.1 add_convert_fusion.2.refs_4_.mine_ref
  89.6 0.3 collective-permute-start.11
  89.9 1.6 %place.1 = bf16[448,1024]{1,0:T(8,128)(2,1)} custom-call(s32[7]{0:T(128)S(1)} %stack.31.where, bf16[448,256]{1,0:T(8,128)(2,1)S(1)} %get-tuple-element.29.refs_0_, bf16[448,256]{1,0:T(8,128)(2,1)S(1)} %get-tuple-element.32.refs_1_, bf16[448,128]{1,0:T(8,128)(2,1)S(1)} %collective-permute-done.7.refs_2_, bf16[448,384]{1,0:T(8,128)(2,1)S(1)} %collective-permute-done.9.refs_3_, ...), custom_call_target="tpu_custom_call" | custom-call | tf_op jit(solution)/shard_map/place/pallas_call | solution.py:45
  91.5 3.8 %collective-permute-done.11.theirs_ref = bf16[112,896]{1,0:T(8,128)(2,1)S(1)} collective-permute-done((bf16[112,896]{1,0:T(8,128)(2,1)S(1)}, bf16[112,896]{1,0:T(8,128)(2,1)S(1)}, u32[]{:S(2)}, u32[]{:S(2)}) %collective-permute-start.11) | collective-permute-done | bytes 200736 | tf_op jit(solution)/shard_map/ppermute | solution.py:186
  95.4 1.9 %finish.1 = (f32[3,448,112]{2,1,0:T(8,128)}, f32[3,448,112]{2,1,0:T(8,128)}) custom-call(s32[7]{0:T(128)S(1)} %stack.31.where, bf16[112,896]{1,0:T(8,128)(2,1)S(1)} %add_convert_fusion.2.refs_4_.mine_ref, bf16[112,896]{1,0:T(8,128)(2,1)S(1)} %collective-permute-done.11.theirs_ref), custom_call_target="tpu_custom_call" | custom-call | tf_op jit(solution)/shard_map/finish/pallas_call | solution.py:45
  (3 shorter events, 0.1 us)
Async XLA Ops:
  0.7 1.2 %copy-start = (bf16[1,1024,448]{1,2,0:T(8,128)(2,1)S(1)}, bf16[1,1024,448]{1,2,0:T(8,128)(2,1)}, u32[]{:S(2)}) copy-start(bf16[1,1024,448]{1,2,0:T(8,128)(2,1)} %param.4) | copy-start | bytes 2752516
  1.9 1.2 %copy-start.2 = (bf16[1,1024,448]{1,2,0:T(8,128)(2,1)S(1)}, bf16[1,1024,448]{1,2,0:T(8,128)(2,1)}, u32[]{:S(2)}) copy-start(bf16[1,1024,448]{1,2,0:T(8,128)(2,1)} %param.5) | copy-start | bytes 2752516
  3.1 4.9 %copy-start.4 = (bf16[3,448,112]{2,1,0:T(8,128)(2,1)S(1)}, bf16[3,448,112]{2,1,0:T(8,128)(2,1)}, u32[]{:S(2)}) copy-start(bf16[3,448,112]{2,1,0:T(8,128)(2,1)} %w_ref.1) | copy-start | bytes 903172
  3.1 4.9 %copy-start.5 = (bf16[3,448,112]{2,1,0:T(8,128)(2,1)S(1)}, bf16[3,448,112]{2,1,0:T(8,128)(2,1)}, u32[]{:S(2)}) copy-start(bf16[3,448,112]{2,1,0:T(8,128)(2,1)} %w2_ref.1) | copy-start | bytes 903172
  3.8 35.1 %copy-start.1 = (bf16[1,1024,448]{1,2,0:T(8,128)(2,1)S(1)}, bf16[1,1024,448]{1,2,0:T(8,128)(2,1)}, u32[]{:S(2)}) copy-start(bf16[1,1024,448]{1,2,0:T(8,128)(2,1)} %param.4) | copy-start | bytes 2752516
  3.8 35.1 %copy-start.3 = (bf16[1,1024,448]{1,2,0:T(8,128)(2,1)S(1)}, bf16[1,1024,448]{1,2,0:T(8,128)(2,1)}, u32[]{:S(2)}) copy-start(bf16[1,1024,448]{1,2,0:T(8,128)(2,1)} %param.5) | copy-start | bytes 2752516
  3.9 35.1 %collective-permute-start = (bf16[2,448,256]{2,1,0:T(8,128)(2,1)S(1)}, bf16[2,448,256]{2,1,0:T(8,128)(2,1)S(1)}, u32[]{:S(2)}, u32[]{:S(2)}) collective-permute-start(bf16[2,448,256]{2,1,0:T(8,128)(2,1)S(1)} %get-tuple-element.24), channel_id=1, source_target_pairs={{0,8},{4,12},{8,0},{12,4},{1,9},{5,13},{9,1},{13,5},{2,10},{6,14},... | collective-permute-start | bytes 1376264 | tf_op jit(solution)/shard_map/ppermute | solution.py:186
  8.0 40.0 %collective-permute-start.4 = (bf16[2,448,256]{2,1,0:T(8,128)(2,1)S(1)}, bf16[2,448,256]{2,1,0:T(8,128)(2,1)S(1)}, u32[]{:S(2)}, u32[]{:S(2)}) collective-permute-start(bf16[2,448,256]{2,1,0:T(8,128)(2,1)S(1)} %get-tuple-element.25.after_ref), channel_id=1, source_target_pairs={{0,8},{4,12},{8,0},{12,4},{1,9},{5,13},{9,1},{13,5},{2,10},{6,14},... | collective-permute-start | bytes 1376264 | tf_op jit(solution)/shard_map/ppermute | solution.py:186
  8.5 12.6 %collective-permute-start.3 = (bf16[4,112,448]{2,1,0:T(8,128)(2,1)S(1)}, bf16[4,112,448]{2,1,0:T(8,128)(2,1)S(1)}, u32[]{:S(2)}, u32[]{:S(2)}) collective-permute-start(bf16[4,112,448]{2,1,0:T(8,128)(2,1)S(1)} %turn.1.refs_0_), channel_id=1, source_target_pairs={{0,3},{1,2},{2,1},{3,0},{4,7},{5,6},{6,5},{7,4},{8,11},{9,10},{10,... | collective-permute-start | bytes 1204232 | tf_op jit(solution)/shard_map/ppermute | solution.py:186
  9.2 22.0 %collective-permute-start.2 = (bf16[4,112,448]{2,1,0:T(8,128)(2,1)S(1)}, bf16[4,112,448]{2,1,0:T(8,128)(2,1)S(1)}, u32[]{:S(2)}, u32[]{:S(2)}) collective-permute-start(bf16[4,112,448]{2,1,0:T(8,128)(2,1)S(1)} %turn.1.refs_0_), channel_id=1, source_target_pairs={{0,2},{1,3},{2,0},{3,1},{4,6},{5,7},{6,4},{7,5},{8,10},{9,11},{10,... | collective-permute-start | bytes 1204232 | tf_op jit(solution)/shard_map/ppermute | solution.py:186
  10.4 20.8 %collective-permute-start.1 = (bf16[4,112,448]{2,1,0:T(8,128)(2,1)S(1)}, bf16[4,112,448]{2,1,0:T(8,128)(2,1)S(1)}, u32[]{:S(2)}, u32[]{:S(2)}) collective-permute-start(bf16[4,112,448]{2,1,0:T(8,128)(2,1)S(1)} %turn.1.refs_0_), channel_id=1, source_target_pairs={{0,1},{1,0},{2,3},{3,2},{4,5},{5,4},{6,7},{7,6},{8,9},{9,8},{10,11... | collective-permute-start | bytes 1204232 | tf_op jit(solution)/shard_map/ppermute | solution.py:186
  50.8 2.4 %collective-permute-start.5 = (bf16[2,2,112,896]{3,2,1,0:T(8,128)(2,1)S(1)}, bf16[2,2,112,896]{3,2,1,0:T(8,128)(2,1)S(1)}, u32[]{:S(2)}, u32[]{:S(2)}) collective-permute-start(bf16[2,2,112,896]{3,2,1,0:T(8,128)(2,1)S(1)} %get-tuple-element.36), channel_id=1, source_target_pairs={{0,1},{1,0},{2,3},{3,2},{4,5},{5,4},{6,7},{7,6},{8,9},{9,8},{10,11... | collective-permute-start | bytes 2408456 | tf_op jit(solution)/shard_map/ppermute | solution.py:186
  53.4 17.8 %collective-permute-start.6 = (bf16[2,112,896]{2,1,0:T(8,128)(2,1)S(1)}, bf16[2,112,896]{2,1,0:T(8,128)(2,1)S(1)}, u32[]{:S(2)}, u32[]{:S(2)}) collective-permute-start(bf16[2,112,896]{2,1,0:T(8,128)(2,1)S(1)} %get-tuple-element.46), channel_id=1, source_target_pairs={{0,2},{1,3},{2,0},{3,1},{4,6},{5,7},{6,4},{7,5},{8,10},{9,11},{10,... | collective-permute-start | bytes 1204232 | tf_op jit(solution)/shard_map/ppermute | solution.py:186
  55.0 16.2 %collective-permute-start.7 = (bf16[448,128]{1,0:T(8,128)(2,1)S(1)}, bf16[448,128]{1,0:T(8,128)(2,1)S(1)}, u32[]{:S(2)}, u32[]{:S(2)}) collective-permute-start(bf16[448,128]{1,0:T(8,128)(2,1)S(1)} %slice.34), channel_id=1, source_target_pairs={{0,8},{4,12},{8,0},{12,4},{1,9},{5,13},{9,1},{13,5},{2,10},{6,14},... | collective-permute-start | bytes 344072 | tf_op jit(solution)/shard_map/ppermute | solution.py:186
  56.7 21.5 %collective-permute-start.9 = (bf16[448,384]{1,0:T(8,128)(2,1)S(1)}, bf16[448,384]{1,0:T(8,128)(2,1)S(1)}, u32[]{:S(2)}, u32[]{:S(2)}) collective-permute-start(bf16[448,384]{1,0:T(8,128)(2,1)S(1)} %pad_maximum_fusion), channel_id=1, source_target_pairs={{0,8},{4,12},{8,0},{12,4},{1,9},{5,13},{9,1},{13,5},{2,10},{6,14},... | collective-permute-start | bytes 1032200 | tf_op jit(solution)/shard_map/ppermute | solution.py:186
  71.3 9.0 %collective-permute-start.8 = (bf16[112,896]{1,0:T(8,128)(2,1)S(1)}, bf16[112,896]{1,0:T(8,128)(2,1)S(1)}, u32[]{:S(2)}, u32[]{:S(2)}) collective-permute-start(bf16[112,896]{1,0:T(8,128)(2,1)S(1)} %fusion.4), channel_id=1, source_target_pairs={{0,4},{4,0},{8,12},{12,8},{1,5},{5,1},{9,13},{13,9},{2,6},{6,2},{1... | collective-permute-start | bytes 602120 | tf_op jit(solution)/shard_map/ppermute | solution.py:186
  80.3 9.2 %collective-permute-start.10 = (bf16[112,896]{1,0:T(8,128)(2,1)S(1)}, bf16[112,896]{1,0:T(8,128)(2,1)S(1)}, u32[]{:S(2)}, u32[]{:S(2)}) collective-permute-start(bf16[112,896]{1,0:T(8,128)(2,1)S(1)} %fusion.1), channel_id=1, source_target_pairs={{0,8},{4,12},{8,0},{12,4},{1,9},{5,13},{9,1},{13,5},{2,10},{6,14},... | collective-permute-start | bytes 602120 | tf_op jit(solution)/shard_map/ppermute | solution.py:186
  89.6 5.8 %collective-permute-start.11 = (bf16[112,896]{1,0:T(8,128)(2,1)S(1)}, bf16[112,896]{1,0:T(8,128)(2,1)S(1)}, u32[]{:S(2)}, u32[]{:S(2)}) collective-permute-start(bf16[112,896]{1,0:T(8,128)(2,1)S(1)} %add_convert_fusion.2.refs_4_.mine_ref), channel_id=1, source_target_pairs={{0,4},{4,0},{8,12},{12,8},{1,5},{5,1},{9,13},{13,9},{2,6},{6,2},{1... | collective-permute-start | bytes 602120 | tf_op jit(solution)/shard_map/ppermute | solution.py:186

commit v2 on v1

--- a/solution.py
+++ b/solution.py
@@ -10,7 +10,7 @@
 
 FIRST_SHIFT = 2
 SECOND_SHIFT = 4
-CHUNKS = (2, 2)
+CHUNKS = 2
 F32 = jnp.float32
 BF16 = jnp.bfloat16
 
@@ -58,15 +58,13 @@
     return pl.ds(pl.multiple_of(start, 128), size)
 
 
-def pack_kernel(where, x_ref, c_ref, *refs):
-    wires, sems = refs[:-1], refs[-1]
-    copies, start = [], 0
-    for c, wire in enumerate(wires):
-        size = wire.shape[2]
-        for j, ref in enumerate((x_ref, c_ref)):
-            source = ref.at[:, lanes(where[4] + start, size)]
-            copies.append(pltpu.make_async_copy(source, wire.at[j], sems.at[2 * c + j]))
-        start += size
+def pack_kernel(start, where, x_ref, c_ref, *refs):
+    wire_ref, sems = refs[-2:]
+    at = lanes(where[4] + start, wire_ref.shape[2])
+    copies = [
+        pltpu.make_async_copy(ref.at[:, at], wire_ref.at[j], sems.at[j])
+        for j, ref in enumerate((x_ref, c_ref))
+    ]
     for copy in copies:
         copy.start()
     for copy in copies:
@@ -102,47 +100,78 @@
     return jnp.concatenate([o_ref[:, lanes(where[0] + start, size)], wire], axis=1)
 
 
-def ahead_kernel(start, first, last, factor, where, x_ref, c_ref, wire_ref, w_ref, across_ref, *refs):
-    if not first:
-        sums_in, refs = refs[0], refs[1:]
-    mid_ref, refs = refs[0], refs[1:]
+def own_part(where, start, size, x_ref, c_ref, w_ref, across_ref, outs):
+    act_ref, base_ref, cross_ref, delta_ref = outs
+    at = lanes(where[0] + start, size)
+    x = x_ref[:, at].astype(F32)
+    act = gelu_pair(x)[0].astype(BF16)
+    act_ref[...] = act
+    base_ref[...] = x + dot_nn(w_ref[1], act)
+    cross_ref[...] = dot_nn(w_ref[2 - where[1]], act)
+    delta_ref[...] = dot_nn(across_ref[3], c_ref[:, at])
+
+
+def weight_terms(q, cot, act, act_one, mid, size):
+    act_o, act_p = act[:, :size], act[:, size:]
+    mid_o, mid_p = mid[:, :size], mid[:, size:]
+    return ((3, cot, act_one), (1, mid, act), (q, mid_o, act_p), (2 - q, mid_p, act_o))
+
+
+def first_kernel(later, where, x_ref, c_ref, wire_ref, w_ref, across_ref, mid_ref, sums, *outs):
     size = wire_ref.shape[2]
     q = where[1]
-    r = 2 - q
-    x = both(x_ref, where, start, size, wire_ref[0]).astype(F32)
-    cot = both(c_ref, where, start, size, wire_ref[1])
+    x = both(x_ref, where, 0, size, wire_ref[0]).astype(F32)
+    cot = both(c_ref, where, 0, size, wire_ref[1])
     act = gelu_pair(x)[0].astype(BF16)
     act_o, act_p = act[:, :size], act[:, size:]
-    cross = jnp.concatenate([dot_nn(w_ref[q], act_p), dot_nn(w_ref[r], act_o)], axis=1)
+    cross = jnp.concatenate([dot_nn(w_ref[q], act_p), dot_nn(w_ref[2 - q], act_o)], axis=1)
     hidden = (x + dot_nn(w_ref[1], act) + cross).astype(BF16).astype(F32)
     act_one, slope_one = gelu_pair(hidden)
     mid = (cot.astype(F32) + slope_one * dot_nn(across_ref[3], cot)).astype(BF16)
     mid_ref[...] = mid
-    mid_o, mid_p = mid[:, :size], mid[:, size:]
-    terms = (
-        (3, cot, act_one.astype(BF16)),
-        (1, mid, act),
-        (q, mid_o, act_p),
-        (r, mid_p, act_o),
-    )
-    if not last:
-        (sums,) = refs
-        for k, left, right in terms:
-            value = dot_nt(left, right)
-            sums[k] = value if first else sums_in[k] + value
-        return
-    keep_ref, give_ref, total = refs
-    for k, left, right in terms:
-        total[k] = ((sums_in[k] + dot_nt(left, right)) * factor).astype(BF16)
-    shard = keep_ref.shape[2]
-    for ref, core in ((keep_ref, where[2]), (give_ref, 1 - where[2])):
+    for k, left, right in weight_terms(q, cot, act, act_one.astype(BF16), mid, size):
+        sums[k] = dot_nt(left, right)
+    own_part(where, size, later, x_ref, c_ref, w_ref, across_ref, outs)
+
+
+def last_kernel(start, factor, where, c_ref, wire_ref, w_ref, across_ref, sums, *refs):
+    act_ref, base_ref, cross_ref, delta_ref, mid_ref = refs[:5]
+    outs, total = refs[5:-1], refs[-1]
+    size = wire_ref.shape[2]
+    q = where[1]
+    x_p = wire_ref[0].astype(F32)
+    cot_p = wire_ref[1]
+    act_p = gelu_pair(x_p)[0].astype(BF16)
+    hidden = jnp.concatenate(
+        [
+            base_ref[...] + dot_nn(w_ref[q], act_p),
+            x_p + dot_nn(w_ref[1], act_p) + cross_ref[...],
+        ],
+        axis=1,
+    )
+    act_one, slope_one = gelu_pair(hidden.astype(BF16).astype(F32))
+    cot = both(c_ref, where, start, size, cot_p)
+    delta = jnp.concatenate([delta_ref[...], dot_nn(across_ref[3], cot_p)], axis=1)
+    mid = (cot.astype(F32) + slope_one * delta).astype(BF16)
+    mid_ref[...] = mid
+    act = jnp.concatenate([act_ref[...], act_p], axis=1)
+    for k, left, right in weight_terms(q, cot, act, act_one.astype(BF16), mid, size):
+        total[k] = ((sums[k] + dot_nt(left, right)) * factor).astype(BF16)
+    parts = [ref.shape[2] for ref in outs[::2]]
+    shard = sum(parts)
+    for given in range(2):
+        core = lax.bitwise_xor(where[2], given)
         for j in range(2):
             side = lax.bitwise_xor(where[6], 1 - j)
             rows = pl.ds(pl.multiple_of((2 * side + core) * shard, 16), shard)
             for k in range(2):
                 level = lax.bitwise_xor(where[5], 1 - k)
                 pair = [total[level, rows, :], total[level + 2, rows, :]]
-                ref[j, k] = jnp.concatenate(pair, axis=1)
+                pair = jnp.concatenate(pair, axis=1)
+                first = 0
+                for h, part in enumerate(parts):
+                    outs[2 * h + given][j, k] = pair[first : first + part]
+                    first += part
 
 
 def back_kernel(start, where, x_ref, wire_ref, mid_ref, across_ref, own_ref, give_ref):
@@ -159,26 +188,85 @@
     give_ref[...] = grad[:, size:]
 
 
-def finish_kernel(where, mine_ref, theirs_ref, one_ref, two_ref):
-    chans = one_ref.shape[1]
-    even = where[5] == 0
-    mine, theirs = mine_ref[...], theirs_ref[...]
-    for want, taps in ((even, ((one_ref, 0), (one_ref, 2))), (~even, ((one_ref, 1), (two_ref, 1)))):
-        terms = jnp.where(want, mine, theirs).astype(F32)
-        for j, (out, k) in enumerate(taps):
-            out[k] = terms[:, j * chans : (j + 1) * chans].T
-    two_ref[0] = jnp.zeros(two_ref.shape[1:], F32)
-    two_ref[2] = jnp.zeros(two_ref.shape[1:], F32)
-
-
-def place_kernel(where, *refs):
-    out_ref, refs = refs[-1], refs[:-2]
-    count = len(CHUNKS)
-    for base, pieces in ((where[0], refs[:count]), (where[4], refs[count:])):
-        start = 0
-        for ref in pieces:
-            out_ref[:, lanes(base + start, ref.shape[1])] = ref[...]
-            start += ref.shape[1]
+def finish_kernel(other, where, *refs):
+    (one_ref, two_ref), (turned, zeros, sems) = refs[-5:-3], refs[-3:]
+    terms = refs[: len(refs) - 5 - (2 if other else 0)]
+    chans = turned.shape[1]
+    if not other:
+        zeros[...] = jnp.zeros(zeros.shape, F32)
+        blank = [pltpu.make_async_copy(zeros, two_ref.at[k], sems.at[2 + k]) for k in (0, 2)]
+        for copy in blank:
+            copy.start()
+    rows = jnp.concatenate([ref[...].astype(F32) for ref in terms], axis=0)
+    for j in range(2):
+        turned[j] = rows[:, j * chans : (j + 1) * chans].T
+    parity = lax.bitwise_xor(where[5], 1) if other else where[5]
+    for want, places in ((0, ((one_ref, 0), (one_ref, 2))), (1, ((one_ref, 1), (two_ref, 1)))):
+
+        @pl.when(parity == want)
+        def _():
+            copies = [
+                pltpu.make_async_copy(turned.at[j], ref.at[k], sems.at[j])
+                for j, (ref, k) in enumerate(places)
+            ]
+            for copy in copies:
+                copy.start()
+            for copy in copies:
+                copy.wait()
+
+    if not other:
+        for copy in blank:
+            copy.wait()
+
+
+def finished(where, terms, chans, shard, held=()):
+    return call(
+        functools.partial(finish_kernel, bool(held)),
+        "finish",
+        [((3, chans, shard), F32)] * 2,
+        [where, *terms, *held],
+        [SMEM] + [VMEM] * len(terms) + [HBM] * len(held),
+        out_specs=[HBM, HBM],
+        scratch=[
+            pltpu.VMEM((2, chans, shard), F32),
+            pltpu.VMEM((chans, shard), F32),
+            pltpu.SemaphoreType.DMA((5,)),
+        ],
+        aliases={len(terms) + 1 + j: j for j in range(len(held))},
+    )
+
+
+def place_kernel(plan, where, *refs):
+    pieces, (out_ref, sems) = refs[: len(plan)], refs[-2:]
+    copies = [
+        pltpu.make_async_copy(
+            ref,
+            out_ref.at[pl.ds(row, ref.shape[0]), lanes(where[base] + start, ref.shape[1])],
+            sems.at[i],
+        )
+        for i, (ref, (base, row, start)) in enumerate(zip(pieces, plan))
+    ]
+    for copy in copies:
+        copy.start()
+    for copy in copies:
+        copy.wait()
+
+
+def placed(where, plan, pieces, shape, after):
+    (out,) = call(
+        functools.partial(place_kernel, plan),
+        "place",
+        [(shape, BF16)],
+        [where, *pieces, after],
+        [SMEM] + [VMEM] * len(pieces) + [ANY],
+        out_specs=[HBM],
+        scratch=[pltpu.SemaphoreType.DMA((len(pieces),))],
+    )
+    return out
+
+
+def in_hbm(value):
+    return pltpu.with_memory_space_constraint(value, pltpu.HBM)
 
 
 def swapped(value, axis, bit):
@@ -195,7 +283,7 @@
     block = inputs.shape[1]
     shard = chans // 4
     half = block // 2
-    sizes = [half * part // sum(CHUNKS) for part in CHUNKS]
+    sizes = [half // CHUNKS] * CHUNKS
     factor = 1.0 / math.sqrt(
         inputs.shape[0] * lax.axis_size("dp") * inputs.shape[1] * lax.axis_size("seq")
     )
@@ -207,20 +295,23 @@
     where = where.astype(jnp.int32)
     x, cot = inputs.reshape(block, chans).T, cotangent.reshape(block, chans).T
 
-    packed = call(
-        pack_kernel,
-        "pack",
-        [((2, chans, size), BF16) for size in sizes],
-        [where, x, cot],
-        [SMEM, HBM, HBM],
-        scratch=[pltpu.SemaphoreType.DMA((2 * len(sizes),))],
-    )
+    packed, start = [], 0
+    for size in sizes:
+        packed += call(
+            functools.partial(pack_kernel, start),
+            "pack",
+            [((2, chans, size), BF16)],
+            [where, in_hbm(x), in_hbm(cot)] + packed[-1:],
+            [SMEM, HBM, HBM] + [ANY] * len(packed[-1:]),
+            scratch=[pltpu.SemaphoreType.DMA((2,))],
+        )
+        start += size
     wires = [swapped(wire, "seq", FIRST_SHIFT) for wire in packed]
     (own_shard,) = call(
         turn_kernel,
         "turn",
         [((4, shard, chans), BF16)],
-        [first_weight_matrix, weight_two, packed[-1]],
+        [in_hbm(first_weight_matrix), in_hbm(weight_two), packed[-1]],
         [HBM, HBM, ANY],
         scratch=[pltpu.VMEM((4, chans, shard), BF16), pltpu.SemaphoreType.DMA((2,))],
     )
@@ -233,62 +324,72 @@
         [SMEM] + [VMEM] * 4,
     )
 
-    start, sums, own, back = 0, [], [], []
-    for c, size in enumerate(sizes):
-        last = c == len(sizes) - 1
-        out = [((chans, 2 * size), BF16)]
-        out += [((2, 2, shard, 2 * chans), BF16)] * 2 if last else [((4, chans, chans), F32)]
-        operands = [where, x, cot, wires[c], w, across] + sums
-        mid, *rest = call(
-            functools.partial(ahead_kernel, start, c == 0, last, factor),
-            f"ahead_{c}",
-            out,
-            operands,
-            [SMEM] + [VMEM] * (len(operands) - 1),
-            scratch=[pltpu.VMEM((4, chans, chans), BF16)] if last else [],
-            aliases={6: 1} if sums and not last else {},
-        )
-        if last:
-            keep, give = rest
-        else:
-            sums = rest
-        mine, theirs = call(
-            functools.partial(back_kernel, start),
+    def backward(c, mid):
+        return call(
+            functools.partial(back_kernel, c * size),
             f"back_{c}",
             [((chans, size), BF16)] * 2,
             [where, x, wires[c], mid, across],
             [SMEM] + [VMEM] * 4,
         )
-        own.append(mine)
-        back.append(theirs)
-        start += size
-
-    back[0], give = lax.optimization_barrier((back[0], give))
-    whole = jnp.concatenate(back, axis=1)
-    returned = [swapped(part, "seq", FIRST_SHIFT) for part in (whole[:, :128], whole[:, 128:])]
-    got_core = swapped(give, "dp", 1)
-    theirs = swapped(added(keep[0], got_core[0]), "dp", 2)
-    mine = added(keep[1], got_core[1])
-    theirs, returned[0] = lax.optimization_barrier((theirs, returned[0]))
-    theirs, mine = added(mine[0], theirs[0]), added(mine[1], theirs[1])
-    theirs, returned[1] = lax.optimization_barrier((swapped(theirs, "seq", 1), returned[1]))
-    mine = added(mine, theirs)
-    mine = added(mine, swapped(mine, "seq", 2))
-    theirs = swapped(mine, "seq", 1)
-    (input_grad,) = call(
-        place_kernel,
-        "place",
-        [((chans, block), BF16)],
-        [where, *own, *returned, mine],
-        [SMEM] + [VMEM] * (len(own) + len(returned)) + [ANY],
-    )
-    grad_one, grad_two = call(
-        finish_kernel,
-        "finish",
-        [((3, chans, shard), F32)] * 2,
-        [where, mine, theirs],
-        [SMEM, VMEM, VMEM],
-    )
+
+    size = half // CHUNKS
+    own = []
+    mid, *held = call(
+        functools.partial(first_kernel, size),
+        "first",
+        [((chans, 2 * size), BF16), ((4, chans, chans), F32), ((chans, size), BF16)]
+        + [((chans, size), F32)] * 3,
+        [where, x, cot, wires[0], w, across],
+        [SMEM] + [VMEM] * 5,
+    )
+    mine, theirs = backward(0, mid)
+    own.append(mine)
+    back = [theirs]
+    back[0], wires[1] = lax.optimization_barrier((back[0], wires[1]))
+    mid, *halves = call(
+        functools.partial(last_kernel, size, factor),
+        "last",
+        [((chans, 2 * size), BF16)]
+        + [((2, 2, shard // 2, 2 * chans), BF16)] * 4,
+        [where, cot, wires[1], w, across, *held],
+        [SMEM] + [VMEM] * 9,
+        scratch=[pltpu.VMEM((4, chans, chans), BF16)],
+    )
+
+    tie = lambda *values: list(lax.optimization_barrier(values))
+    keep, give = halves[0::2], halves[1::2]
+    returned = [swapped(back[0], "seq", FIRST_SHIFT)]
+    got = [swapped(v, "dp", 1) for v in give]
+    send = [added(k[0], v[0]) for k, v in zip(keep, got)]
+    mine = [added(k[1], v[1]) for k, v in zip(keep, got)]
+    send[0], mid = tie(send[0], mid)
+    own_last, theirs = backward(1, mid)
+    own.append(own_last)
+    cut = chans // 2
+    first, second = theirs[:cut], theirs[cut:]
+    send = tie(*send)
+    got = [swapped(v, "dp", 2) for v in send]
+    got[1], first = tie(got[1], first)
+    returned.append(swapped(first, "seq", FIRST_SHIFT))
+    send = [added(m[0], v[0]) for m, v in zip(mine, got)]
+    mine = [added(m[1], v[1]) for m, v in zip(mine, got)]
+    send[0], mine[1] = tie(send[0], mine[1])
+    got = [swapped(v, "seq", 1) for v in send]
+    got[0], second = tie(got[0], second)
+    returned.append(swapped(second, "seq", FIRST_SHIFT))
+    mine = [added(m, v) for m, v in zip(mine, got)]
+    mine = [added(m, swapped(m, "seq", 2)) for m in mine]
+    theirs = [swapped(m, "seq", 1) for m in mine]
+    input_grad = placed(
+        where,
+        ((0, 0, 0), (0, 0, size), (4, 0, 0), (4, 0, size), (4, cut, size)),
+        own + returned,
+        (chans, block),
+        mine[1],
+    )
+    held = finished(where, mine, chans, shard)
+    grad_one, grad_two = finished(where, theirs, chans, shard, held)
     return (input_grad.T.reshape(inputs.shape), grad_one, grad_two)
 
 
@@ -378,7 +479,7 @@
         and seq <= SECOND_SHIFT
         and dp == 4
         and inputs.shape[0] == 1
-        and inputs.shape[1] % (256 * sum(CHUNKS)) == 0
+        and inputs.shape[1] % (256 * CHUNKS) == 0
     ):
         return on_pairs(inputs, *others)
     return on_shifts(inputs, *others)

time: 97.5 us -> 88.7 us (0.910)
  waiting for transfers between devices: 67.5 us -> 48.1 us
  starting transfers between devices: 11.7 us -> 19.9 us
  Pallas kernels: 14.4 us -> 19.2 us
  local copies, waits for them, and re-layouts: 2.47 us -> 0.11 us
    ppermute x12 -> x18, waiting for transfers between devices: 67.5 us -> 48.1 us  [swapped(): return lax.ppermute(value, axis, route)]
    ppermute x12 -> x18, starting transfers between devices: 11.7 us -> 19.9 us  [swapped(): return lax.ppermute(value, axis, route)]
    pallas_call x9 -> x11, Pallas kernels: 14.4 us -> 19.2 us  [call(): pl.pallas_call(body, out_shape=[jax.ShapeDtypeStruct(*o) for o in out], i...]
    unnamed x12 -> x4, local copies, waits for them, and re-layouts: 2.38 us -> 0.01 us
  transfers between devices with their start and end apart: 12 -> 18, of which waited for: 10 -> 12; matrix products, arithmetic and copies ran while one was open for 0% -> 0% of each run, Pallas kernels for 9% -> 15%
where the time goes in v2:
time: 88.7 us; the launch traced here: 88.6 us
  waiting for transfers between devices  48.1 us (54%)
  starting transfers between devices  19.9 us (22%)
  Pallas kernels  19.2 us (22%)
    ppermute x18, waiting for transfers between devices, swapped(): return lax.ppermute(value, axis, route)  48.1 us
    ppermute x18, starting transfers between devices, swapped(): return lax.ppermute(value, axis, route)  19.9 us
    pallas_call x11, Pallas kernels, call(): pl.pallas_call(body, out_shape=[jax.ShapeDtypeStruct(*o) for o in out], i...  19.2 us
  transfers between devices with their start and end apart: 18, of which 12 were waited for; matrix products, arithmetic and copies ran while one was open for 0% of the time, Pallas kernels for 15%

profile of v2, /device:TPU:0, one launch (start us, length us, event | category | flops | bytes accessed | tf_op | source)
XLA Modules:
  0.0 88.6 jit_solution(3820758652819457559)
XLA Ops:
  0.7 0.1 stack.31.where
  0.7 1.6 %pack.2.refs_0_ = bf16[2,448,256]{2,1,0:T(8,128)(2,1)S(1)} custom-call(s32[7]{0:T(128)S(1)} %stack.31.where, bf16[448,1024]{1,0:T(8,128)(2,1)} %bitcast.51, bf16[448,1024]{1,0:T(8,128)(2,1)} %bitcast.56), custom_call_target="tpu_custom_call" | custom-call | tf_op jit(solution)/shard_map/pack/pallas_call | solution.py:45
  2.4 4.1 %collective-permute-start = (bf16[2,448,256]{2,1,0:T(8,128)(2,1)S(1)}, bf16[2,448,256]{2,1,0:T(8,128)(2,1)S(1)}, u32[]{:S(2)}, u32[]{:S(2)}) collective-permute-start(bf16[2,448,256]{2,1,0:T(8,128)(2,1)S(1)} %pack.2.refs_0_), channel_id=1, source_target_pairs={{0,8},{4,12},{8,0},{12,4},{1,9},{5,13},{9,1},{13,5},{2,10},{6,14},... | collective-permute-start | bytes 1376264 | tf_op jit(solution)/shard_map/ppermute | solution.py:274
  6.5 1.6 %pack.3.after_ref = bf16[2,448,256]{2,1,0:T(8,128)(2,1)S(1)} custom-call(s32[7]{0:T(128)S(1)} %stack.31.where, bf16[448,1024]{1,0:T(8,128)(2,1)} %bitcast.52, bf16[448,1024]{1,0:T(8,128)(2,1)} %bitcast.57, bf16[2,448,256]{2,1,0:T(8,128)(2,1)S(1)} %pack.2.refs_0_), custom_call_target="tpu_custom_call" | custom-call | tf_op jit(solution)/shard_map/pack/pallas_call | solution.py:45
  8.1 0.0 copy-start
  8.1 0.0 copy-start.1
  8.1 0.1 collective-permute-start.4
  8.2 1.3 %turn.1.refs_0_ = bf16[4,112,448]{2,1,0:T(8,128)(2,1)S(1)} custom-call(bf16[3,448,112]{2,1,0:T(8,128)(2,1)} %w_ref.1, bf16[3,448,112]{2,1,0:T(8,128)(2,1)} %w2_ref.1, bf16[2,448,256]{2,1,0:T(8,128)(2,1)S(1)} %pack.3.after_ref), custom_call_target="tpu_custom_call" | custom-call | tf_op jit(solution)/shard_map/turn/pallas_call | solution.py:45
  9.5 0.7 collective-permute-start.3
  10.3 1.2 %collective-permute-start.2 = (bf16[4,112,448]{2,1,0:T(8,128)(2,1)S(1)}, bf16[4,112,448]{2,1,0:T(8,128)(2,1)S(1)}, u32[]{:S(2)}, u32[]{:S(2)}) collective-permute-start(bf16[4,112,448]{2,1,0:T(8,128)(2,1)S(1)} %turn.1.refs_0_), channel_id=1, source_target_pairs={{0,2},{1,3},{2,0},{3,1},{4,6},{5,7},{6,4},{7,5},{8,10},{9,11},{10,... | collective-permute-start | bytes 1204232 | tf_op jit(solution)/shard_map/ppermute | solution.py:274
  11.5 0.0 collective-permute-start.1
  11.5 10.6 %collective-permute-done.3.refs_3_ = bf16[4,112,448]{2,1,0:T(8,128)(2,1)S(1)} collective-permute-done((bf16[4,112,448]{2,1,0:T(8,128)(2,1)S(1)}, bf16[4,112,448]{2,1,0:T(8,128)(2,1)S(1)}, u32[]{:S(2)}, u32[]{:S(2)}) %collective-permute-start.3) | collective-permute-done | bytes 401440 | tf_op jit(solution)/shard_map/ppermute | solution.py:274
  22.1 10.1 %collective-permute-done.2.refs_2_ = bf16[4,112,448]{2,1,0:T(8,128)(2,1)S(1)} collective-permute-done((bf16[4,112,448]{2,1,0:T(8,128)(2,1)S(1)}, bf16[4,112,448]{2,1,0:T(8,128)(2,1)S(1)}, u32[]{:S(2)}, u32[]{:S(2)}) %collective-permute-start.2) | collective-permute-done | bytes 401440 | tf_op jit(solution)/shard_map/ppermute | solution.py:274
  32.2 0.0 collective-permute-done.1.refs_1_
  32.2 1.2 %join.1 = (bf16[4,448,448]{2,1,0:T(8,128)(2,1)S(1)}, bf16[4,448,448]{2,1,0:T(8,128)(2,1)S(1)}) custom-call(s32[7]{0:T(128)S(1)} %stack.31.where, bf16[4,112,448]{2,1,0:T(8,128)(2,1)S(1)} %turn.1.refs_0_, bf16[4,112,448]{2,1,0:T(8,128)(2,1)S(1)} %collective-permute-done.1.refs_1_, bf16[4,112,448]{2,1,0:T(8,128)(2,1)S(1)} %collective-permute-done.2.refs_2_, ...), custom_call_target="tpu_custom_call" | custom-call | tf_op jit(solution)/shard_map/join/pallas_call | solution.py:45
  33.5 4.0 %collective-permute-done.wire_ref = bf16[2,448,256]{2,1,0:T(8,128)(2,1)S(1)} collective-permute-done((bf16[2,448,256]{2,1,0:T(8,128)(2,1)S(1)}, bf16[2,448,256]{2,1,0:T(8,128)(2,1)S(1)}, u32[]{:S(2)}, u32[]{:S(2)}) %collective-permute-start) | collective-permute-done | bytes 458784 | tf_op jit(solution)/shard_map/ppermute | solution.py:274
  37.5 0.0 copy-done
  37.5 0.0 copy-done.1
  37.5 2.9 %first.1 = (bf16[448,512]{1,0:T(8,128)(2,1)S(1)}, f32[4,448,448]{2,1,0:T(8,128)S(1)}, bf16[448,256]{1,0:T(8,128)(2,1)S(1)}, f32[448,256]{1,0:T(8,128)S(1)}, f32[...) custom-call(s32[7]{0:T(128)S(1)} %stack.31.where, bf16[448,1024]{1,0:T(8,128)(2,1)S(1)} %bitcast.53, ...), custom_call_target="tpu_custom_call" | custom-call | tf_op jit(solution)/shard_map/first/pallas_call | solution.py:45
  40.4 1.5 %back_0.1 = (bf16[448,256]{1,0:T(8,128)(2,1)S(1)}, bf16[448,256]{1,0:T(8,128)(2,1)S(1)}) custom-call(s32[7]{0:T(128)S(1)} %stack.31.where, bf16[448,1024]{1,0:T(8,128)(2,1)S(1)} %bitcast.54, bf16[2,448,256]{2,1,0:T(8,128)(2,1)S(1)} %collective-permute-done.wire_ref, bf16[448,512]{1,0:T(8,128)(2,1)S(1)} %get-tuple-element.38.mid_ref, ...), custom_call_target="tpu_custom_call" | custom-call | tf_op jit(solution)/shard_map/back_0/pallas_call | solution.py:45
  42.0 4.5 %collective-permute-done.4.wire_ref = bf16[2,448,256]{2,1,0:T(8,128)(2,1)S(1)} collective-permute-done((bf16[2,448,256]{2,1,0:T(8,128)(2,1)S(1)}, bf16[2,448,256]{2,1,0:T(8,128)(2,1)S(1)}, u32[]{:S(2)}, u32[]{:S(2)}) %collective-permute-start.4) | collective-permute-done | bytes 458784 | tf_op jit(solution)/shard_map/ppermute | solution.py:274
  46.5 2.7 %last.1 = (bf16[448,512]{1,0:T(8,128)(2,1)S(1)}, bf16[2,2,56,896]{3,2,1,0:T(8,128)(2,1)S(1)}, bf16[2,2,56,896]{3,2,1,0:T(8,128)(2,1)S(1)}, bf16[2,2,56,896]{3,2,...) custom-call(s32[7]{0:T(128)S(1)} %stack.31.where, bf16[448,1024]{1,0:T(8,128)(2,1)S(1)} %bitcast.59, ...), custom_call_target="tpu_custom_call" | custom-call | tf_op jit(solution)/shard_map/last/pallas_call | solution.py:45
  49.2 0.1 collective-permute-start.5
  49.3 0.5 collective-permute-start.7
  49.8 0.0 collective-permute-start.6
  49.8 1.2 %collective-permute-done.5 = bf16[2,2,56,896]{3,2,1,0:T(8,128)(2,1)S(1)} collective-permute-done((bf16[2,2,56,896]{3,2,1,0:T(8,128)(2,1)S(1)}, bf16[2,2,56,896]{3,2,1,0:T(8,128)(2,1)S(1)}, u32[]{:S(2)}, u32[]{:S(2)}) %collective-permute-start.5) | collective-permute-done | bytes 401440 | tf_op jit(solution)/shard_map/ppermute | solution.py:274
  51.0 0.1 add_convert_fusion.1
  51.1 1.6 %back_1.1 = (bf16[448,256]{1,0:T(8,128)(2,1)S(1)}, bf16[448,256]{1,0:T(8,128)(2,1)S(1)}) custom-call(s32[7]{0:T(128)S(1)} %stack.31.where, bf16[448,1024]{1,0:T(8,128)(2,1)S(1)} %bitcast.55, bf16[2,448,256]{2,1,0:T(8,128)(2,1)S(1)} %collective-permute-done.4.wire_ref, bf16[448,512]{1,0:T(8,128)(2,1)S(1)} %get-tuple-element.50.mid_ref, ...), custom_call_target="tpu_custom_call" | custom-call | tf_op jit(solution)/shard_map/back_1/pallas_call | solution.py:45
  52.7 0.0 collective-permute-done.7
  52.7 0.1 add_convert_fusion
  52.8 1.6 %collective-permute-start.8 = (bf16[2,56,896]{2,1,0:T(8,128)(2,1)S(1)}, bf16[2,56,896]{2,1,0:T(8,128)(2,1)S(1)}, u32[]{:S(2)}, u32[]{:S(2)}) collective-permute-start(bf16[2,56,896]{2,1,0:T(8,128)(2,1)S(1)} %get-tuple-element.56), channel_id=1, source_target_pairs={{0,2},{1,3},{2,0},{3,1},{4,6},{5,7},{6,4},{7,5},{8,10},{9,11},{10,... | collective-permute-start | bytes 602120 | tf_op jit(solution)/shard_map/ppermute | solution.py:274
  54.4 0.5 collective-permute-start.10
  54.9 5.8 %collective-permute-done.8 = bf16[2,56,896]{2,1,0:T(8,128)(2,1)S(1)} collective-permute-done((bf16[2,56,896]{2,1,0:T(8,128)(2,1)S(1)}, bf16[2,56,896]{2,1,0:T(8,128)(2,1)S(1)}, u32[]{:S(2)}, u32[]{:S(2)}) %collective-permute-start.8) | collective-permute-done | bytes 200736 | tf_op jit(solution)/shard_map/ppermute | solution.py:274
  60.7 0.1 fusion.9
  60.7 3.0 %collective-permute-start.13 = (bf16[56,896]{1,0:T(8,128)(2,1)S(1)}, bf16[56,896]{1,0:T(8,128)(2,1)S(1)}, u32[]{:S(2)}, u32[]{:S(2)}) collective-permute-start(bf16[56,896]{1,0:T(8,128)(2,1)S(1)} %get-tuple-element.73), channel_id=1, source_target_pairs={{0,4},{4,0},{8,12},{12,8},{1,5},{5,1},{9,13},{13,9},{2,6},{6,2},{1... | collective-permute-start | bytes 301064 | tf_op jit(solution)/shard_map/ppermute | solution.py:274
  63.7 1.2 %collective-permute-start.9 = (bf16[224,256]{1,0:T(8,128)(2,1)S(1)}, bf16[224,256]{1,0:T(8,128)(2,1)S(1)}, u32[]{:S(2)}, u32[]{:S(2)}) collective-permute-start(bf16[224,256]{1,0:T(8,128)(2,1)S(1)} %get-tuple-element.58), channel_id=1, source_target_pairs={{0,8},{4,12},{8,0},{12,4},{1,9},{5,13},{9,1},{13,5},{2,10},{6,14},... | collective-permute-start | bytes 344072 | tf_op jit(solution)/shard_map/ppermute | solution.py:274
  64.9 0.0 collective-permute-done.10
  64.9 1.9 %collective-permute-start.11 = (bf16[56,896]{1,0:T(8,128)(2,1)S(1)}, bf16[56,896]{1,0:T(8,128)(2,1)S(1)}, u32[]{:S(2)}, u32[]{:S(2)}) collective-permute-start(bf16[56,896]{1,0:T(8,128)(2,1)S(1)} %fusion.7), channel_id=1, source_target_pairs={{0,4},{4,0},{8,12},{12,8},{1,5},{5,1},{9,13},{13,9},{2,6},{6,2},{1... | collective-permute-start | bytes 301064 | tf_op jit(solution)/shard_map/ppermute | solution.py:274
  66.8 0.7 collective-permute-done.13
  67.5 1.0 %collective-permute-start.14 = (bf16[56,896]{1,0:T(8,128)(2,1)S(1)}, bf16[56,896]{1,0:T(8,128)(2,1)S(1)}, u32[]{:S(2)}, u32[]{:S(2)}) collective-permute-start(bf16[56,896]{1,0:T(8,128)(2,1)S(1)} %add_convert_fusion.6), channel_id=1, source_target_pairs={{0,8},{4,12},{8,0},{12,4},{1,9},{5,13},{9,1},{13,5},{2,10},{6,14},... | collective-permute-start | bytes 301064 | tf_op jit(solution)/shard_map/ppermute | solution.py:274
  68.5 2.6 %collective-permute-done.11 = bf16[56,896]{1,0:T(8,128)(2,1)S(1)} collective-permute-done((bf16[56,896]{1,0:T(8,128)(2,1)S(1)}, bf16[56,896]{1,0:T(8,128)(2,1)S(1)}, u32[]{:S(2)}, u32[]{:S(2)}) %collective-permute-start.11) | collective-permute-done | bytes 100384 | tf_op jit(solution)/shard_map/ppermute | solution.py:274
  71.1 1.6 %collective-permute-start.15 = (bf16[56,896]{1,0:T(8,128)(2,1)S(1)}, bf16[56,896]{1,0:T(8,128)(2,1)S(1)}, u32[]{:S(2)}, u32[]{:S(2)}) collective-permute-start(bf16[56,896]{1,0:T(8,128)(2,1)S(1)} %fusion.2), channel_id=1, source_target_pairs={{0,8},{4,12},{8,0},{12,4},{1,9},{5,13},{9,1},{13,5},{2,10},{6,14},... | collective-permute-start | bytes 301064 | tf_op jit(solution)/shard_map/ppermute | solution.py:274
  72.7 1.4 %collective-permute-start.12 = (bf16[224,256]{1,0:T(8,128)(2,1)S(1)}, bf16[224,256]{1,0:T(8,128)(2,1)S(1)}, u32[]{:S(2)}, u32[]{:S(2)}) collective-permute-start(bf16[224,256]{1,0:T(8,128)(2,1)S(1)} %get-tuple-element.62), channel_id=1, source_target_pairs={{0,8},{4,12},{8,0},{12,4},{1,9},{5,13},{9,1},{13,5},{2,10},{6,14},... | collective-permute-start | bytes 344072 | tf_op jit(solution)/shard_map/ppermute | solution.py:274
  74.1 4.4 %collective-permute-done.14 = bf16[56,896]{1,0:T(8,128)(2,1)S(1)} collective-permute-done((bf16[56,896]{1,0:T(8,128)(2,1)S(1)}, bf16[56,896]{1,0:T(8,128)(2,1)S(1)}, u32[]{:S(2)}, u32[]{:S(2)}) %collective-permute-start.14) | collective-permute-done | bytes 100384 | tf_op jit(solution)/shard_map/ppermute | solution.py:274
  78.6 1.0 %collective-permute-start.17 = (bf16[56,896]{1,0:T(8,128)(2,1)S(1)}, bf16[56,896]{1,0:T(8,128)(2,1)S(1)}, u32[]{:S(2)}, u32[]{:S(2)}) collective-permute-start(bf16[56,896]{1,0:T(8,128)(2,1)S(1)} %add_convert_fusion.5.refs_5_.refs_1_), channel_id=1, source_target_pairs={{0,4},{4,0},{8,12},{12,8},{1,5},{5,1},{9,13},{13,9},{2,6},{6,2},{1... | collective-permute-start | bytes 301064 | tf_op jit(solution)/shard_map/ppermute | solution.py:274
  79.6 2.6 %collective-permute-done.15 = bf16[56,896]{1,0:T(8,128)(2,1)S(1)} collective-permute-done((bf16[56,896]{1,0:T(8,128)(2,1)S(1)}, bf16[56,896]{1,0:T(8,128)(2,1)S(1)}, u32[]{:S(2)}, u32[]{:S(2)}) %collective-permute-start.15) | collective-permute-done | bytes 100384 | tf_op jit(solution)/shard_map/ppermute | solution.py:274
  82.2 0.1 collective-permute-start.16
  82.3 1.6 %finish.2 = (f32[3,448,112]{2,1,0:T(8,128)}, f32[3,448,112]{2,1,0:T(8,128)}) custom-call(s32[7]{0:T(128)S(1)} %stack.31.where, bf16[56,896]{1,0:T(8,128)(2,1)S(1)} %add_convert_fusion.4.refs_0_, bf16[56,896]{1,0:T(8,128)(2,1)S(1)} %add_convert_fusion.5.refs_5_.refs_1_), custom_call_target="tpu_custom_call" | custom-call | tf_op jit(solution)/shard_map/finish/pallas_call | solution.py:45
  83.9 0.0 collective-permute-done.6.refs_2_
  83.9 0.0 collective-permute-done.9.refs_3_
  83.9 0.0 collective-permute-done.12.refs_4_
  83.9 1.5 %place.1 = bf16[448,1024]{1,0:T(8,128)(2,1)} custom-call(s32[7]{0:T(128)S(1)} %stack.31.where, bf16[448,256]{1,0:T(8,128)(2,1)S(1)} %get-tuple-element.39.refs_0_, bf16[448,256]{1,0:T(8,128)(2,1)S(1)} %get-tuple-element.51.refs_1_, bf16[448,256]{1,0:T(8,128)(2,1)S(1)} %collective-permute-done.6.refs_2_, bf16[224,256]{1,0:T(8,128)(2,1)S(1)} %collective-permute-done.9.refs_3_, ...), custom_call_target="tpu_custom_call" | custom-call | tf_op jit(solution)/shard_map/place/pallas_call | solution.py:45
  85.4 0.4 collective-permute-done.17.refs_1_
  85.8 1.2 %collective-permute-done.16.refs_0_ = bf16[56,896]{1,0:T(8,128)(2,1)S(1)} collective-permute-done((bf16[56,896]{1,0:T(8,128)(2,1)S(1)}, bf16[56,896]{1,0:T(8,128)(2,1)S(1)}, u32[]{:S(2)}, u32[]{:S(2)}) %collective-permute-start.16) | collective-permute-done | bytes 100384 | tf_op jit(solution)/shard_map/ppermute | solution.py:274
  87.0 1.6 %finish.3 = (f32[3,448,112]{2,1,0:T(8,128)}, f32[3,448,112]{2,1,0:T(8,128)}) custom-call(s32[7]{0:T(128)S(1)} %stack.31.where, bf16[56,896]{1,0:T(8,128)(2,1)S(1)} %collective-permute-done.16.refs_0_, bf16[56,896]{1,0:T(8,128)(2,1)S(1)} %collective-permute-done.17.refs_1_, ...), custom_call_target="tpu_custom_call", output_to_operand_aliasing={{0}: (3, {}), {1}: (4, {})} | custom-call | tf_op jit(solution)/shard_map/finish/pallas_call | solution.py:45
  (6 shorter events, 0.2 us)
Async XLA Ops:
  2.4 35.1 %collective-permute-start = (bf16[2,448,256]{2,1,0:T(8,128)(2,1)S(1)}, bf16[2,448,256]{2,1,0:T(8,128)(2,1)S(1)}, u32[]{:S(2)}, u32[]{:S(2)}) collective-permute-start(bf16[2,448,256]{2,1,0:T(8,128)(2,1)S(1)} %pack.2.refs_0_), channel_id=1, source_target_pairs={{0,8},{4,12},{8,0},{12,4},{1,9},{5,13},{9,1},{13,5},{2,10},{6,14},... | collective-permute-start | bytes 1376264 | tf_op jit(solution)/shard_map/ppermute | solution.py:274
  8.1 29.4 %copy-start = (bf16[1,1024,448]{1,2,0:T(8,128)(2,1)S(1)}, bf16[1,1024,448]{1,2,0:T(8,128)(2,1)}, u32[]{:S(2)}) copy-start(bf16[1,1024,448]{1,2,0:T(8,128)(2,1)} %param.4) | copy-start | bytes 2752516
  8.1 29.4 %copy-start.1 = (bf16[1,1024,448]{1,2,0:T(8,128)(2,1)S(1)}, bf16[1,1024,448]{1,2,0:T(8,128)(2,1)}, u32[]{:S(2)}) copy-start(bf16[1,1024,448]{1,2,0:T(8,128)(2,1)} %param.5) | copy-start | bytes 2752516
  8.1 38.4 %collective-permute-start.4 = (bf16[2,448,256]{2,1,0:T(8,128)(2,1)S(1)}, bf16[2,448,256]{2,1,0:T(8,128)(2,1)S(1)}, u32[]{:S(2)}, u32[]{:S(2)}) collective-permute-start(bf16[2,448,256]{2,1,0:T(8,128)(2,1)S(1)} %pack.3.after_ref), channel_id=1, source_target_pairs={{0,8},{4,12},{8,0},{12,4},{1,9},{5,13},{9,1},{13,5},{2,10},{6,14},... | collective-permute-start | bytes 1376264 | tf_op jit(solution)/shard_map/ppermute | solution.py:274
  9.5 12.6 %collective-permute-start.3 = (bf16[4,112,448]{2,1,0:T(8,128)(2,1)S(1)}, bf16[4,112,448]{2,1,0:T(8,128)(2,1)S(1)}, u32[]{:S(2)}, u32[]{:S(2)}) collective-permute-start(bf16[4,112,448]{2,1,0:T(8,128)(2,1)S(1)} %turn.1.refs_0_), channel_id=1, source_target_pairs={{0,3},{1,2},{2,1},{3,0},{4,7},{5,6},{6,5},{7,4},{8,11},{9,10},{10,... | collective-permute-start | bytes 1204232 | tf_op jit(solution)/shard_map/ppermute | solution.py:274
  10.3 22.0 %collective-permute-start.2 = (bf16[4,112,448]{2,1,0:T(8,128)(2,1)S(1)}, bf16[4,112,448]{2,1,0:T(8,128)(2,1)S(1)}, u32[]{:S(2)}, u32[]{:S(2)}) collective-permute-start(bf16[4,112,448]{2,1,0:T(8,128)(2,1)S(1)} %turn.1.refs_0_), channel_id=1, source_target_pairs={{0,2},{1,3},{2,0},{3,1},{4,6},{5,7},{6,4},{7,5},{8,10},{9,11},{10,... | collective-permute-start | bytes 1204232 | tf_op jit(solution)/shard_map/ppermute | solution.py:274
  11.5 20.8 %collective-permute-start.1 = (bf16[4,112,448]{2,1,0:T(8,128)(2,1)S(1)}, bf16[4,112,448]{2,1,0:T(8,128)(2,1)S(1)}, u32[]{:S(2)}, u32[]{:S(2)}) collective-permute-start(bf16[4,112,448]{2,1,0:T(8,128)(2,1)S(1)} %turn.1.refs_0_), channel_id=1, source_target_pairs={{0,1},{1,0},{2,3},{3,2},{4,5},{5,4},{6,7},{7,6},{8,9},{9,8},{10,11... | collective-permute-start | bytes 1204232 | tf_op jit(solution)/shard_map/ppermute | solution.py:274
  49.2 1.8 %collective-permute-start.5 = (bf16[2,2,56,896]{3,2,1,0:T(8,128)(2,1)S(1)}, bf16[2,2,56,896]{3,2,1,0:T(8,128)(2,1)S(1)}, u32[]{:S(2)}, u32[]{:S(2)}) collective-permute-start(bf16[2,2,56,896]{3,2,1,0:T(8,128)(2,1)S(1)} %get-tuple-element.48), channel_id=1, source_target_pairs={{0,1},{1,0},{2,3},{3,2},{4,5},{5,4},{6,7},{7,6},{8,9},{9,8},{10,11... | collective-permute-start | bytes 1204232 | tf_op jit(solution)/shard_map/ppermute | solution.py:274
  49.3 3.4 %collective-permute-start.7 = (bf16[2,2,56,896]{3,2,1,0:T(8,128)(2,1)S(1)}, bf16[2,2,56,896]{3,2,1,0:T(8,128)(2,1)S(1)}, u32[]{:S(2)}, u32[]{:S(2)}) collective-permute-start(bf16[2,2,56,896]{3,2,1,0:T(8,128)(2,1)S(1)} %get-tuple-element.55), channel_id=1, source_target_pairs={{0,1},{1,0},{2,3},{3,2},{4,5},{5,4},{6,7},{7,6},{8,9},{9,8},{10,11... | collective-permute-start | bytes 1204232 | tf_op jit(solution)/shard_map/ppermute | solution.py:274
  49.8 34.1 %collective-permute-start.6 = (bf16[448,256]{1,0:T(8,128)(2,1)S(1)}, bf16[448,256]{1,0:T(8,128)(2,1)S(1)}, u32[]{:S(2)}, u32[]{:S(2)}) collective-permute-start(bf16[448,256]{1,0:T(8,128)(2,1)S(1)} %get-tuple-element.52), channel_id=1, source_target_pairs={{0,8},{4,12},{8,0},{12,4},{1,9},{5,13},{9,1},{13,5},{2,10},{6,14},... | collective-permute-start | bytes 688136 | tf_op jit(solution)/shard_map/ppermute | solution.py:274
  52.8 7.9 %collective-permute-start.8 = (bf16[2,56,896]{2,1,0:T(8,128)(2,1)S(1)}, bf16[2,56,896]{2,1,0:T(8,128)(2,1)S(1)}, u32[]{:S(2)}, u32[]{:S(2)}) collective-permute-start(bf16[2,56,896]{2,1,0:T(8,128)(2,1)S(1)} %get-tuple-element.56), channel_id=1, source_target_pairs={{0,2},{1,3},{2,0},{3,1},{4,6},{5,7},{6,4},{7,5},{8,10},{9,11},{10,... | collective-permute-start | bytes 602120 | tf_op jit(solution)/shard_map/ppermute | solution.py:274
  54.4 10.5 %collective-permute-start.10 = (bf16[2,56,896]{2,1,0:T(8,128)(2,1)S(1)}, bf16[2,56,896]{2,1,0:T(8,128)(2,1)S(1)}, u32[]{:S(2)}, u32[]{:S(2)}) collective-permute-start(bf16[2,56,896]{2,1,0:T(8,128)(2,1)S(1)} %get-tuple-element.59), channel_id=1, source_target_pairs={{0,2},{1,3},{2,0},{3,1},{4,6},{5,7},{6,4},{7,5},{8,10},{9,11},{10,... | collective-permute-start | bytes 602120 | tf_op jit(solution)/shard_map/ppermute | solution.py:274
  60.7 6.7 %collective-permute-start.13 = (bf16[56,896]{1,0:T(8,128)(2,1)S(1)}, bf16[56,896]{1,0:T(8,128)(2,1)S(1)}, u32[]{:S(2)}, u32[]{:S(2)}) collective-permute-start(bf16[56,896]{1,0:T(8,128)(2,1)S(1)} %get-tuple-element.73), channel_id=1, source_target_pairs={{0,4},{4,0},{8,12},{12,8},{1,5},{5,1},{9,13},{13,9},{2,6},{6,2},{1... | collective-permute-start | bytes 301064 | tf_op jit(solution)/shard_map/ppermute | solution.py:274
  63.7 20.2 %collective-permute-start.9 = (bf16[224,256]{1,0:T(8,128)(2,1)S(1)}, bf16[224,256]{1,0:T(8,128)(2,1)S(1)}, u32[]{:S(2)}, u32[]{:S(2)}) collective-permute-start(bf16[224,256]{1,0:T(8,128)(2,1)S(1)} %get-tuple-element.58), channel_id=1, source_target_pairs={{0,8},{4,12},{8,0},{12,4},{1,9},{5,13},{9,1},{13,5},{2,10},{6,14},... | collective-permute-start | bytes 344072 | tf_op jit(solution)/shard_map/ppermute | solution.py:274
  64.9 6.1 %collective-permute-start.11 = (bf16[56,896]{1,0:T(8,128)(2,1)S(1)}, bf16[56,896]{1,0:T(8,128)(2,1)S(1)}, u32[]{:S(2)}, u32[]{:S(2)}) collective-permute-start(bf16[56,896]{1,0:T(8,128)(2,1)S(1)} %fusion.7), channel_id=1, source_target_pairs={{0,4},{4,0},{8,12},{12,8},{1,5},{5,1},{9,13},{13,9},{2,6},{6,2},{1... | collective-permute-start | bytes 301064 | tf_op jit(solution)/shard_map/ppermute | solution.py:274
  67.5 11.1 %collective-permute-start.14 = (bf16[56,896]{1,0:T(8,128)(2,1)S(1)}, bf16[56,896]{1,0:T(8,128)(2,1)S(1)}, u32[]{:S(2)}, u32[]{:S(2)}) collective-permute-start(bf16[56,896]{1,0:T(8,128)(2,1)S(1)} %add_convert_fusion.6), channel_id=1, source_target_pairs={{0,8},{4,12},{8,0},{12,4},{1,9},{5,13},{9,1},{13,5},{2,10},{6,14},... | collective-permute-start | bytes 301064 | tf_op jit(solution)/shard_map/ppermute | solution.py:274
  71.1 11.0 %collective-permute-start.15 = (bf16[56,896]{1,0:T(8,128)(2,1)S(1)}, bf16[56,896]{1,0:T(8,128)(2,1)S(1)}, u32[]{:S(2)}, u32[]{:S(2)}) collective-permute-start(bf16[56,896]{1,0:T(8,128)(2,1)S(1)} %fusion.2), channel_id=1, source_target_pairs={{0,8},{4,12},{8,0},{12,4},{1,9},{5,13},{9,1},{13,5},{2,10},{6,14},... | collective-permute-start | bytes 301064 | tf_op jit(solution)/shard_map/ppermute | solution.py:274
  72.7 11.2 %collective-permute-start.12 = (bf16[224,256]{1,0:T(8,128)(2,1)S(1)}, bf16[224,256]{1,0:T(8,128)(2,1)S(1)}, u32[]{:S(2)}, u32[]{:S(2)}) collective-permute-start(bf16[224,256]{1,0:T(8,128)(2,1)S(1)} %get-tuple-element.62), channel_id=1, source_target_pairs={{0,8},{4,12},{8,0},{12,4},{1,9},{5,13},{9,1},{13,5},{2,10},{6,14},... | collective-permute-start | bytes 344072 | tf_op jit(solution)/shard_map/ppermute | solution.py:274
  78.6 7.3 %collective-permute-start.17 = (bf16[56,896]{1,0:T(8,128)(2,1)S(1)}, bf16[56,896]{1,0:T(8,128)(2,1)S(1)}, u32[]{:S(2)}, u32[]{:S(2)}) collective-permute-start(bf16[56,896]{1,0:T(8,128)(2,1)S(1)} %add_convert_fusion.5.refs_5_.refs_1_), channel_id=1, source_target_pairs={{0,4},{4,0},{8,12},{12,8},{1,5},{5,1},{9,13},{13,9},{2,6},{6,2},{1... | collective-permute-start | bytes 301064 | tf_op jit(solution)/shard_map/ppermute | solution.py:274
  82.2 4.8 %collective-permute-start.16 = (bf16[56,896]{1,0:T(8,128)(2,1)S(1)}, bf16[56,896]{1,0:T(8,128)(2,1)S(1)}, u32[]{:S(2)}, u32[]{:S(2)}) collective-permute-start(bf16[56,896]{1,0:T(8,128)(2,1)S(1)} %add_convert_fusion.4.refs_0_), channel_id=1, source_target_pairs={{0,4},{4,0},{8,12},{12,8},{1,5},{5,1},{9,13},{13,9},{2,6},{6,2},{1... | collective-permute-start | bytes 301064 | tf_op jit(solution)/shard_map/ppermute | solution.py:274

commit v3 on v2

--- a/solution.py
+++ b/solution.py
@@ -134,6 +134,15 @@
     own_part(where, size, later, x_ref, c_ref, w_ref, across_ref, outs)
 
 
+def row_parts(shard):
+    main = shard // 32 * 16
+    rest = shard // 2 - main
+    return (
+        (slice(0, main), slice(2 * main, 2 * main + rest)),
+        (slice(main, 2 * main), slice(2 * main + rest, shard)),
+    )
+
+
 def last_kernel(start, factor, where, c_ref, wire_ref, w_ref, across_ref, sums, *refs):
     act_ref, base_ref, cross_ref, delta_ref, mid_ref = refs[:5]
     outs, total = refs[5:-1], refs[-1]
@@ -157,8 +166,7 @@
     act = jnp.concatenate([act_ref[...], act_p], axis=1)
     for k, left, right in weight_terms(q, cot, act, act_one.astype(BF16), mid, size):
         total[k] = ((sums[k] + dot_nt(left, right)) * factor).astype(BF16)
-    parts = [ref.shape[2] for ref in outs[::2]]
-    shard = sum(parts)
+    shard = 2 * outs[0].shape[2]
     for given in range(2):
         core = lax.bitwise_xor(where[2], given)
         for j in range(2):
@@ -168,10 +176,10 @@
                 level = lax.bitwise_xor(where[5], 1 - k)
                 pair = [total[level, rows, :], total[level + 2, rows, :]]
                 pair = jnp.concatenate(pair, axis=1)
-                first = 0
-                for h, part in enumerate(parts):
-                    outs[2 * h + given][j, k] = pair[first : first + part]
-                    first += part
+                for h, (main, rest) in enumerate(row_parts(shard)):
+                    out = outs[2 * h + given]
+                    out[j, k, : main.stop - main.start] = pair[main]
+                    out[j, k, main.stop - main.start :] = pair[rest]
 
 
 def back_kernel(start, where, x_ref, wire_ref, mid_ref, across_ref, own_ref, give_ref):
@@ -197,7 +205,9 @@
         blank = [pltpu.make_async_copy(zeros, two_ref.at[k], sems.at[2 + k]) for k in (0, 2)]
         for copy in blank:
             copy.start()
-    rows = jnp.concatenate([ref[...].astype(F32) for ref in terms], axis=0)
+    halves = [ref[...].astype(F32) for ref in terms]
+    main = turned.shape[2] // 32 * 16
+    rows = jnp.concatenate([v[:main] for v in halves] + [v[main:] for v in halves], axis=0)
     for j in range(2):
         turned[j] = rows[:, j * chans : (j + 1) * chans].T
     parity = lax.bitwise_xor(where[5], 1) if other else where[5]
@@ -386,7 +396,7 @@
         ((0, 0, 0), (0, 0, size), (4, 0, 0), (4, 0, size), (4, cut, size)),
         own + returned,
         (chans, block),
-        mine[1],
+        mine[0],
     )
     held = finished(where, mine, chans, shard)
     grad_one, grad_two = finished(where, theirs, chans, shard, held)

time: 88.7 us -> 88.8 us (level)
  no operation moved by 1% of the time
where the time goes in v3:
time: 88.8 us; the launch traced here: 88.6 us
  waiting for transfers between devices  48.1 us (54%)
  starting transfers between devices  19.9 us (22%)
  Pallas kernels  19.2 us (22%)
    ppermute x18, waiting for transfers between devices, swapped(): return lax.ppermute(value, axis, route)  48.1 us
    ppermute x18, starting transfers between devices, swapped(): return lax.ppermute(value, axis, route)  19.9 us
    pallas_call x11, Pallas kernels, call(): pl.pallas_call(body, out_shape=[jax.ShapeDtypeStruct(*o) for o in out], i...  19.2 us
  transfers between devices with their start and end apart: 18, of which 12 were waited for; matrix products, arithmetic and copies ran while one was open for 0% of the time, Pallas kernels for 15%

profile of v3, /device:TPU:0, one launch (start us, length us, event | category | flops | bytes accessed | tf_op | source)
XLA Modules:
  0.0 88.6 jit_solution(2481376851816559959)
XLA Ops:
  0.7 0.1 stack.31.where
  0.7 1.6 %pack.2.refs_0_ = bf16[2,448,256]{2,1,0:T(8,128)(2,1)S(1)} custom-call(s32[7]{0:T(128)S(1)} %stack.31.where, bf16[448,1024]{1,0:T(8,128)(2,1)} %bitcast.51, bf16[448,1024]{1,0:T(8,128)(2,1)} %bitcast.56), custom_call_target="tpu_custom_call" | custom-call | tf_op jit(solution)/shard_map/pack/pallas_call | solution.py:45
  2.4 4.1 %collective-permute-start = (bf16[2,448,256]{2,1,0:T(8,128)(2,1)S(1)}, bf16[2,448,256]{2,1,0:T(8,128)(2,1)S(1)}, u32[]{:S(2)}, u32[]{:S(2)}) collective-permute-start(bf16[2,448,256]{2,1,0:T(8,128)(2,1)S(1)} %pack.2.refs_0_), channel_id=1, source_target_pairs={{0,8},{4,12},{8,0},{12,4},{1,9},{5,13},{9,1},{13,5},{2,10},{6,14},... | collective-permute-start | bytes 1376264 | tf_op jit(solution)/shard_map/ppermute | solution.py:284
  6.5 1.6 %pack.3.after_ref = bf16[2,448,256]{2,1,0:T(8,128)(2,1)S(1)} custom-call(s32[7]{0:T(128)S(1)} %stack.31.where, bf16[448,1024]{1,0:T(8,128)(2,1)} %bitcast.52, bf16[448,1024]{1,0:T(8,128)(2,1)} %bitcast.57, bf16[2,448,256]{2,1,0:T(8,128)(2,1)S(1)} %pack.2.refs_0_), custom_call_target="tpu_custom_call" | custom-call | tf_op jit(solution)/shard_map/pack/pallas_call | solution.py:45
  8.1 0.0 copy-start
  8.1 0.0 copy-start.1
  8.1 0.1 collective-permute-start.4
  8.2 1.3 %turn.1.refs_0_ = bf16[4,112,448]{2,1,0:T(8,128)(2,1)S(1)} custom-call(bf16[3,448,112]{2,1,0:T(8,128)(2,1)} %w_ref.1, bf16[3,448,112]{2,1,0:T(8,128)(2,1)} %w2_ref.1, bf16[2,448,256]{2,1,0:T(8,128)(2,1)S(1)} %pack.3.after_ref), custom_call_target="tpu_custom_call" | custom-call | tf_op jit(solution)/shard_map/turn/pallas_call | solution.py:45
  9.5 0.7 collective-permute-start.3
  10.3 1.2 %collective-permute-start.2 = (bf16[4,112,448]{2,1,0:T(8,128)(2,1)S(1)}, bf16[4,112,448]{2,1,0:T(8,128)(2,1)S(1)}, u32[]{:S(2)}, u32[]{:S(2)}) collective-permute-start(bf16[4,112,448]{2,1,0:T(8,128)(2,1)S(1)} %turn.1.refs_0_), channel_id=1, source_target_pairs={{0,2},{1,3},{2,0},{3,1},{4,6},{5,7},{6,4},{7,5},{8,10},{9,11},{10,... | collective-permute-start | bytes 1204232 | tf_op jit(solution)/shard_map/ppermute | solution.py:284
  11.5 0.0 collective-permute-start.1
  11.5 10.6 %collective-permute-done.3.refs_3_ = bf16[4,112,448]{2,1,0:T(8,128)(2,1)S(1)} collective-permute-done((bf16[4,112,448]{2,1,0:T(8,128)(2,1)S(1)}, bf16[4,112,448]{2,1,0:T(8,128)(2,1)S(1)}, u32[]{:S(2)}, u32[]{:S(2)}) %collective-permute-start.3) | collective-permute-done | bytes 401440 | tf_op jit(solution)/shard_map/ppermute | solution.py:284
  22.1 10.1 %collective-permute-done.2.refs_2_ = bf16[4,112,448]{2,1,0:T(8,128)(2,1)S(1)} collective-permute-done((bf16[4,112,448]{2,1,0:T(8,128)(2,1)S(1)}, bf16[4,112,448]{2,1,0:T(8,128)(2,1)S(1)}, u32[]{:S(2)}, u32[]{:S(2)}) %collective-permute-start.2) | collective-permute-done | bytes 401440 | tf_op jit(solution)/shard_map/ppermute | solution.py:284
  32.2 0.0 collective-permute-done.1.refs_1_
  32.2 1.2 %join.1 = (bf16[4,448,448]{2,1,0:T(8,128)(2,1)S(1)}, bf16[4,448,448]{2,1,0:T(8,128)(2,1)S(1)}) custom-call(s32[7]{0:T(128)S(1)} %stack.31.where, bf16[4,112,448]{2,1,0:T(8,128)(2,1)S(1)} %turn.1.refs_0_, bf16[4,112,448]{2,1,0:T(8,128)(2,1)S(1)} %collective-permute-done.1.refs_1_, bf16[4,112,448]{2,1,0:T(8,128)(2,1)S(1)} %collective-permute-done.2.refs_2_, ...), custom_call_target="tpu_custom_call" | custom-call | tf_op jit(solution)/shard_map/join/pallas_call | solution.py:45
  33.5 4.0 %collective-permute-done.wire_ref = bf16[2,448,256]{2,1,0:T(8,128)(2,1)S(1)} collective-permute-done((bf16[2,448,256]{2,1,0:T(8,128)(2,1)S(1)}, bf16[2,448,256]{2,1,0:T(8,128)(2,1)S(1)}, u32[]{:S(2)}, u32[]{:S(2)}) %collective-permute-start) | collective-permute-done | bytes 458784 | tf_op jit(solution)/shard_map/ppermute | solution.py:284
  37.5 0.0 copy-done
  37.5 0.0 copy-done.1
  37.5 2.9 %first.1 = (bf16[448,512]{1,0:T(8,128)(2,1)S(1)}, f32[4,448,448]{2,1,0:T(8,128)S(1)}, bf16[448,256]{1,0:T(8,128)(2,1)S(1)}, f32[448,256]{1,0:T(8,128)S(1)}, f32[...) custom-call(s32[7]{0:T(128)S(1)} %stack.31.where, bf16[448,1024]{1,0:T(8,128)(2,1)S(1)} %bitcast.53, ...), custom_call_target="tpu_custom_call" | custom-call | tf_op jit(solution)/shard_map/first/pallas_call | solution.py:45
  40.4 1.5 %back_0.1 = (bf16[448,256]{1,0:T(8,128)(2,1)S(1)}, bf16[448,256]{1,0:T(8,128)(2,1)S(1)}) custom-call(s32[7]{0:T(128)S(1)} %stack.31.where, bf16[448,1024]{1,0:T(8,128)(2,1)S(1)} %bitcast.54, bf16[2,448,256]{2,1,0:T(8,128)(2,1)S(1)} %collective-permute-done.wire_ref, bf16[448,512]{1,0:T(8,128)(2,1)S(1)} %get-tuple-element.38.mid_ref, ...), custom_call_target="tpu_custom_call" | custom-call | tf_op jit(solution)/shard_map/back_0/pallas_call | solution.py:45
  42.0 4.5 %collective-permute-done.4.wire_ref = bf16[2,448,256]{2,1,0:T(8,128)(2,1)S(1)} collective-permute-done((bf16[2,448,256]{2,1,0:T(8,128)(2,1)S(1)}, bf16[2,448,256]{2,1,0:T(8,128)(2,1)S(1)}, u32[]{:S(2)}, u32[]{:S(2)}) %collective-permute-start.4) | collective-permute-done | bytes 458784 | tf_op jit(solution)/shard_map/ppermute | solution.py:284
  46.5 2.7 %last.1 = (bf16[448,512]{1,0:T(8,128)(2,1)S(1)}, bf16[2,2,56,896]{3,2,1,0:T(8,128)(2,1)S(1)}, bf16[2,2,56,896]{3,2,1,0:T(8,128)(2,1)S(1)}, bf16[2,2,56,896]{3,2,...) custom-call(s32[7]{0:T(128)S(1)} %stack.31.where, bf16[448,1024]{1,0:T(8,128)(2,1)S(1)} %bitcast.59, ...), custom_call_target="tpu_custom_call" | custom-call | tf_op jit(solution)/shard_map/last/pallas_call | solution.py:45
  49.2 0.1 collective-permute-start.5
  49.3 0.5 collective-permute-start.7
  49.8 0.0 collective-permute-start.6
  49.8 1.2 %collective-permute-done.5 = bf16[2,2,56,896]{3,2,1,0:T(8,128)(2,1)S(1)} collective-permute-done((bf16[2,2,56,896]{3,2,1,0:T(8,128)(2,1)S(1)}, bf16[2,2,56,896]{3,2,1,0:T(8,128)(2,1)S(1)}, u32[]{:S(2)}, u32[]{:S(2)}) %collective-permute-start.5) | collective-permute-done | bytes 401440 | tf_op jit(solution)/shard_map/ppermute | solution.py:284
  51.0 0.1 add_convert_fusion.1
  51.1 1.6 %back_1.1 = (bf16[448,256]{1,0:T(8,128)(2,1)S(1)}, bf16[448,256]{1,0:T(8,128)(2,1)S(1)}) custom-call(s32[7]{0:T(128)S(1)} %stack.31.where, bf16[448,1024]{1,0:T(8,128)(2,1)S(1)} %bitcast.55, bf16[2,448,256]{2,1,0:T(8,128)(2,1)S(1)} %collective-permute-done.4.wire_ref, bf16[448,512]{1,0:T(8,128)(2,1)S(1)} %get-tuple-element.50.mid_ref, ...), custom_call_target="tpu_custom_call" | custom-call | tf_op jit(solution)/shard_map/back_1/pallas_call | solution.py:45
  52.7 0.0 collective-permute-done.7
  52.7 0.1 add_convert_fusion
  52.8 1.6 %collective-permute-start.8 = (bf16[2,56,896]{2,1,0:T(8,128)(2,1)S(1)}, bf16[2,56,896]{2,1,0:T(8,128)(2,1)S(1)}, u32[]{:S(2)}, u32[]{:S(2)}) collective-permute-start(bf16[2,56,896]{2,1,0:T(8,128)(2,1)S(1)} %get-tuple-element.56), channel_id=1, source_target_pairs={{0,2},{1,3},{2,0},{3,1},{4,6},{5,7},{6,4},{7,5},{8,10},{9,11},{10,... | collective-permute-start | bytes 602120 | tf_op jit(solution)/shard_map/ppermute | solution.py:284
  54.4 0.5 collective-permute-start.10
  54.9 5.8 %collective-permute-done.8 = bf16[2,56,896]{2,1,0:T(8,128)(2,1)S(1)} collective-permute-done((bf16[2,56,896]{2,1,0:T(8,128)(2,1)S(1)}, bf16[2,56,896]{2,1,0:T(8,128)(2,1)S(1)}, u32[]{:S(2)}, u32[]{:S(2)}) %collective-permute-start.8) | collective-permute-done | bytes 200736 | tf_op jit(solution)/shard_map/ppermute | solution.py:284
  60.7 0.1 fusion.10
  60.7 3.0 %collective-permute-start.15 = (bf16[56,896]{1,0:T(8,128)(2,1)S(1)}, bf16[56,896]{1,0:T(8,128)(2,1)S(1)}, u32[]{:S(2)}, u32[]{:S(2)}) collective-permute-start(bf16[56,896]{1,0:T(8,128)(2,1)S(1)} %get-tuple-element.73), channel_id=1, source_target_pairs={{0,4},{4,0},{8,12},{12,8},{1,5},{5,1},{9,13},{13,9},{2,6},{6,2},{1... | collective-permute-start | bytes 301064 | tf_op jit(solution)/shard_map/ppermute | solution.py:284
  63.7 1.2 %collective-permute-start.9 = (bf16[224,256]{1,0:T(8,128)(2,1)S(1)}, bf16[224,256]{1,0:T(8,128)(2,1)S(1)}, u32[]{:S(2)}, u32[]{:S(2)}) collective-permute-start(bf16[224,256]{1,0:T(8,128)(2,1)S(1)} %get-tuple-element.58), channel_id=1, source_target_pairs={{0,8},{4,12},{8,0},{12,4},{1,9},{5,13},{9,1},{13,5},{2,10},{6,14},... | collective-permute-start | bytes 344072 | tf_op jit(solution)/shard_map/ppermute | solution.py:284
  64.9 0.0 collective-permute-done.10
  64.9 1.9 %collective-permute-start.11 = (bf16[56,896]{1,0:T(8,128)(2,1)S(1)}, bf16[56,896]{1,0:T(8,128)(2,1)S(1)}, u32[]{:S(2)}, u32[]{:S(2)}) collective-permute-start(bf16[56,896]{1,0:T(8,128)(2,1)S(1)} %fusion.7), channel_id=1, source_target_pairs={{0,4},{4,0},{8,12},{12,8},{1,5},{5,1},{9,13},{13,9},{2,6},{6,2},{1... | collective-permute-start | bytes 301064 | tf_op jit(solution)/shard_map/ppermute | solution.py:284
  66.8 0.7 collective-permute-done.15
  67.5 1.0 %collective-permute-start.16 = (bf16[56,896]{1,0:T(8,128)(2,1)S(1)}, bf16[56,896]{1,0:T(8,128)(2,1)S(1)}, u32[]{:S(2)}, u32[]{:S(2)}) collective-permute-start(bf16[56,896]{1,0:T(8,128)(2,1)S(1)} %add_convert_fusion.5), channel_id=1, source_target_pairs={{0,8},{4,12},{8,0},{12,4},{1,9},{5,13},{9,1},{13,5},{2,10},{6,14},... | collective-permute-start | bytes 301064 | tf_op jit(solution)/shard_map/ppermute | solution.py:284
  68.5 2.6 %collective-permute-done.11 = bf16[56,896]{1,0:T(8,128)(2,1)S(1)} collective-permute-done((bf16[56,896]{1,0:T(8,128)(2,1)S(1)}, bf16[56,896]{1,0:T(8,128)(2,1)S(1)}, u32[]{:S(2)}, u32[]{:S(2)}) %collective-permute-start.11) | collective-permute-done | bytes 100384 | tf_op jit(solution)/shard_map/ppermute | solution.py:284
  71.1 1.6 %collective-permute-start.13 = (bf16[56,896]{1,0:T(8,128)(2,1)S(1)}, bf16[56,896]{1,0:T(8,128)(2,1)S(1)}, u32[]{:S(2)}, u32[]{:S(2)}) collective-permute-start(bf16[56,896]{1,0:T(8,128)(2,1)S(1)} %fusion.3), channel_id=1, source_target_pairs={{0,8},{4,12},{8,0},{12,4},{1,9},{5,13},{9,1},{13,5},{2,10},{6,14},... | collective-permute-start | bytes 301064 | tf_op jit(solution)/shard_map/ppermute | solution.py:284
  72.7 1.4 %collective-permute-start.12 = (bf16[224,256]{1,0:T(8,128)(2,1)S(1)}, bf16[224,256]{1,0:T(8,128)(2,1)S(1)}, u32[]{:S(2)}, u32[]{:S(2)}) collective-permute-start(bf16[224,256]{1,0:T(8,128)(2,1)S(1)} %get-tuple-element.62), channel_id=1, source_target_pairs={{0,8},{4,12},{8,0},{12,4},{1,9},{5,13},{9,1},{13,5},{2,10},{6,14},... | collective-permute-start | bytes 344072 | tf_op jit(solution)/shard_map/ppermute | solution.py:284
  74.1 4.4 %collective-permute-done.16 = bf16[56,896]{1,0:T(8,128)(2,1)S(1)} collective-permute-done((bf16[56,896]{1,0:T(8,128)(2,1)S(1)}, bf16[56,896]{1,0:T(8,128)(2,1)S(1)}, u32[]{:S(2)}, u32[]{:S(2)}) %collective-permute-start.16) | collective-permute-done | bytes 100384 | tf_op jit(solution)/shard_map/ppermute | solution.py:284
  78.6 1.0 %collective-permute-start.17 = (bf16[56,896]{1,0:T(8,128)(2,1)S(1)}, bf16[56,896]{1,0:T(8,128)(2,1)S(1)}, u32[]{:S(2)}, u32[]{:S(2)}) collective-permute-start(bf16[56,896]{1,0:T(8,128)(2,1)S(1)} %add_convert_fusion.4.refs_1_), channel_id=1, source_target_pairs={{0,4},{4,0},{8,12},{12,8},{1,5},{5,1},{9,13},{13,9},{2,6},{6,2},{1... | collective-permute-start | bytes 301064 | tf_op jit(solution)/shard_map/ppermute | solution.py:284
  79.6 2.6 %collective-permute-done.13 = bf16[56,896]{1,0:T(8,128)(2,1)S(1)} collective-permute-done((bf16[56,896]{1,0:T(8,128)(2,1)S(1)}, bf16[56,896]{1,0:T(8,128)(2,1)S(1)}, u32[]{:S(2)}, u32[]{:S(2)}) %collective-permute-start.13) | collective-permute-done | bytes 100384 | tf_op jit(solution)/shard_map/ppermute | solution.py:284
  82.2 0.1 collective-permute-start.14
  82.3 1.6 %finish.2 = (f32[3,448,112]{2,1,0:T(8,128)}, f32[3,448,112]{2,1,0:T(8,128)}) custom-call(s32[7]{0:T(128)S(1)} %stack.31.where, bf16[56,896]{1,0:T(8,128)(2,1)S(1)} %add_convert_fusion.6.refs_5_.refs_0_, bf16[56,896]{1,0:T(8,128)(2,1)S(1)} %add_convert_fusion.4.refs_1_), custom_call_target="tpu_custom_call" | custom-call | tf_op jit(solution)/shard_map/finish/pallas_call | solution.py:45
  83.9 0.0 collective-permute-done.6.refs_2_
  83.9 0.0 collective-permute-done.9.refs_3_
  83.9 0.0 collective-permute-done.12.refs_4_
  83.9 1.5 %place.1 = bf16[448,1024]{1,0:T(8,128)(2,1)} custom-call(s32[7]{0:T(128)S(1)} %stack.31.where, bf16[448,256]{1,0:T(8,128)(2,1)S(1)} %get-tuple-element.39.refs_0_, bf16[448,256]{1,0:T(8,128)(2,1)S(1)} %get-tuple-element.51.refs_1_, bf16[448,256]{1,0:T(8,128)(2,1)S(1)} %collective-permute-done.6.refs_2_, bf16[224,256]{1,0:T(8,128)(2,1)S(1)} %collective-permute-done.9.refs_3_, ...), custom_call_target="tpu_custom_call" | custom-call | tf_op jit(solution)/shard_map/place/pallas_call | solution.py:45
  85.4 0.4 collective-permute-done.17.refs_1_
  85.8 1.2 %collective-permute-done.14.refs_0_ = bf16[56,896]{1,0:T(8,128)(2,1)S(1)} collective-permute-done((bf16[56,896]{1,0:T(8,128)(2,1)S(1)}, bf16[56,896]{1,0:T(8,128)(2,1)S(1)}, u32[]{:S(2)}, u32[]{:S(2)}) %collective-permute-start.14) | collective-permute-done | bytes 100384 | tf_op jit(solution)/shard_map/ppermute | solution.py:284
  87.0 1.6 %finish.3 = (f32[3,448,112]{2,1,0:T(8,128)}, f32[3,448,112]{2,1,0:T(8,128)}) custom-call(s32[7]{0:T(128)S(1)} %stack.31.where, bf16[56,896]{1,0:T(8,128)(2,1)S(1)} %collective-permute-done.14.refs_0_, bf16[56,896]{1,0:T(8,128)(2,1)S(1)} %collective-permute-done.17.refs_1_, ...), custom_call_target="tpu_custom_call", output_to_operand_aliasing={{0}: (3, {}), {1}: (4, {})} | custom-call | tf_op jit(solution)/shard_map/finish/pallas_call | solution.py:45
  (6 shorter events, 0.2 us)
Async XLA Ops:
  2.4 35.1 %collective-permute-start = (bf16[2,448,256]{2,1,0:T(8,128)(2,1)S(1)}, bf16[2,448,256]{2,1,0:T(8,128)(2,1)S(1)}, u32[]{:S(2)}, u32[]{:S(2)}) collective-permute-start(bf16[2,448,256]{2,1,0:T(8,128)(2,1)S(1)} %pack.2.refs_0_), channel_id=1, source_target_pairs={{0,8},{4,12},{8,0},{12,4},{1,9},{5,13},{9,1},{13,5},{2,10},{6,14},... | collective-permute-start | bytes 1376264 | tf_op jit(solution)/shard_map/ppermute | solution.py:284
  8.1 29.4 %copy-start = (bf16[1,1024,448]{1,2,0:T(8,128)(2,1)S(1)}, bf16[1,1024,448]{1,2,0:T(8,128)(2,1)}, u32[]{:S(2)}) copy-start(bf16[1,1024,448]{1,2,0:T(8,128)(2,1)} %param.4) | copy-start | bytes 2752516
  8.1 29.4 %copy-start.1 = (bf16[1,1024,448]{1,2,0:T(8,128)(2,1)S(1)}, bf16[1,1024,448]{1,2,0:T(8,128)(2,1)}, u32[]{:S(2)}) copy-start(bf16[1,1024,448]{1,2,0:T(8,128)(2,1)} %param.5) | copy-start | bytes 2752516
  8.1 38.4 %collective-permute-start.4 = (bf16[2,448,256]{2,1,0:T(8,128)(2,1)S(1)}, bf16[2,448,256]{2,1,0:T(8,128)(2,1)S(1)}, u32[]{:S(2)}, u32[]{:S(2)}) collective-permute-start(bf16[2,448,256]{2,1,0:T(8,128)(2,1)S(1)} %pack.3.after_ref), channel_id=1, source_target_pairs={{0,8},{4,12},{8,0},{12,4},{1,9},{5,13},{9,1},{13,5},{2,10},{6,14},... | collective-permute-start | bytes 1376264 | tf_op jit(solution)/shard_map/ppermute | solution.py:284
  9.5 12.6 %collective-permute-start.3 = (bf16[4,112,448]{2,1,0:T(8,128)(2,1)S(1)}, bf16[4,112,448]{2,1,0:T(8,128)(2,1)S(1)}, u32[]{:S(2)}, u32[]{:S(2)}) collective-permute-start(bf16[4,112,448]{2,1,0:T(8,128)(2,1)S(1)} %turn.1.refs_0_), channel_id=1, source_target_pairs={{0,3},{1,2},{2,1},{3,0},{4,7},{5,6},{6,5},{7,4},{8,11},{9,10},{10,... | collective-permute-start | bytes 1204232 | tf_op jit(solution)/shard_map/ppermute | solution.py:284
  10.3 22.0 %collective-permute-start.2 = (bf16[4,112,448]{2,1,0:T(8,128)(2,1)S(1)}, bf16[4,112,448]{2,1,0:T(8,128)(2,1)S(1)}, u32[]{:S(2)}, u32[]{:S(2)}) collective-permute-start(bf16[4,112,448]{2,1,0:T(8,128)(2,1)S(1)} %turn.1.refs_0_), channel_id=1, source_target_pairs={{0,2},{1,3},{2,0},{3,1},{4,6},{5,7},{6,4},{7,5},{8,10},{9,11},{10,... | collective-permute-start | bytes 1204232 | tf_op jit(solution)/shard_map/ppermute | solution.py:284
  11.5 20.8 %collective-permute-start.1 = (bf16[4,112,448]{2,1,0:T(8,128)(2,1)S(1)}, bf16[4,112,448]{2,1,0:T(8,128)(2,1)S(1)}, u32[]{:S(2)}, u32[]{:S(2)}) collective-permute-start(bf16[4,112,448]{2,1,0:T(8,128)(2,1)S(1)} %turn.1.refs_0_), channel_id=1, source_target_pairs={{0,1},{1,0},{2,3},{3,2},{4,5},{5,4},{6,7},{7,6},{8,9},{9,8},{10,11... | collective-permute-start | bytes 1204232 | tf_op jit(solution)/shard_map/ppermute | solution.py:284
  49.2 1.8 %collective-permute-start.5 = (bf16[2,2,56,896]{3,2,1,0:T(8,128)(2,1)S(1)}, bf16[2,2,56,896]{3,2,1,0:T(8,128)(2,1)S(1)}, u32[]{:S(2)}, u32[]{:S(2)}) collective-permute-start(bf16[2,2,56,896]{3,2,1,0:T(8,128)(2,1)S(1)} %get-tuple-element.48), channel_id=1, source_target_pairs={{0,1},{1,0},{2,3},{3,2},{4,5},{5,4},{6,7},{7,6},{8,9},{9,8},{10,11... | collective-permute-start | bytes 1204232 | tf_op jit(solution)/shard_map/ppermute | solution.py:284
  49.3 3.4 %collective-permute-start.7 = (bf16[2,2,56,896]{3,2,1,0:T(8,128)(2,1)S(1)}, bf16[2,2,56,896]{3,2,1,0:T(8,128)(2,1)S(1)}, u32[]{:S(2)}, u32[]{:S(2)}) collective-permute-start(bf16[2,2,56,896]{3,2,1,0:T(8,128)(2,1)S(1)} %get-tuple-element.55), channel_id=1, source_target_pairs={{0,1},{1,0},{2,3},{3,2},{4,5},{5,4},{6,7},{7,6},{8,9},{9,8},{10,11... | collective-permute-start | bytes 1204232 | tf_op jit(solution)/shard_map/ppermute | solution.py:284
  49.8 34.1 %collective-permute-start.6 = (bf16[448,256]{1,0:T(8,128)(2,1)S(1)}, bf16[448,256]{1,0:T(8,128)(2,1)S(1)}, u32[]{:S(2)}, u32[]{:S(2)}) collective-permute-start(bf16[448,256]{1,0:T(8,128)(2,1)S(1)} %get-tuple-element.52), channel_id=1, source_target_pairs={{0,8},{4,12},{8,0},{12,4},{1,9},{5,13},{9,1},{13,5},{2,10},{6,14},... | collective-permute-start | bytes 688136 | tf_op jit(solution)/shard_map/ppermute | solution.py:284
  52.8 7.9 %collective-permute-start.8 = (bf16[2,56,896]{2,1,0:T(8,128)(2,1)S(1)}, bf16[2,56,896]{2,1,0:T(8,128)(2,1)S(1)}, u32[]{:S(2)}, u32[]{:S(2)}) collective-permute-start(bf16[2,56,896]{2,1,0:T(8,128)(2,1)S(1)} %get-tuple-element.56), channel_id=1, source_target_pairs={{0,2},{1,3},{2,0},{3,1},{4,6},{5,7},{6,4},{7,5},{8,10},{9,11},{10,... | collective-permute-start | bytes 602120 | tf_op jit(solution)/shard_map/ppermute | solution.py:284
  54.4 10.5 %collective-permute-start.10 = (bf16[2,56,896]{2,1,0:T(8,128)(2,1)S(1)}, bf16[2,56,896]{2,1,0:T(8,128)(2,1)S(1)}, u32[]{:S(2)}, u32[]{:S(2)}) collective-permute-start(bf16[2,56,896]{2,1,0:T(8,128)(2,1)S(1)} %get-tuple-element.59), channel_id=1, source_target_pairs={{0,2},{1,3},{2,0},{3,1},{4,6},{5,7},{6,4},{7,5},{8,10},{9,11},{10,... | collective-permute-start | bytes 602120 | tf_op jit(solution)/shard_map/ppermute | solution.py:284
  60.7 6.7 %collective-permute-start.15 = (bf16[56,896]{1,0:T(8,128)(2,1)S(1)}, bf16[56,896]{1,0:T(8,128)(2,1)S(1)}, u32[]{:S(2)}, u32[]{:S(2)}) collective-permute-start(bf16[56,896]{1,0:T(8,128)(2,1)S(1)} %get-tuple-element.73), channel_id=1, source_target_pairs={{0,4},{4,0},{8,12},{12,8},{1,5},{5,1},{9,13},{13,9},{2,6},{6,2},{1... | collective-permute-start | bytes 301064 | tf_op jit(solution)/shard_map/ppermute | solution.py:284
  63.7 20.2 %collective-permute-start.9 = (bf16[224,256]{1,0:T(8,128)(2,1)S(1)}, bf16[224,256]{1,0:T(8,128)(2,1)S(1)}, u32[]{:S(2)}, u32[]{:S(2)}) collective-permute-start(bf16[224,256]{1,0:T(8,128)(2,1)S(1)} %get-tuple-element.58), channel_id=1, source_target_pairs={{0,8},{4,12},{8,0},{12,4},{1,9},{5,13},{9,1},{13,5},{2,10},{6,14},... | collective-permute-start | bytes 344072 | tf_op jit(solution)/shard_map/ppermute | solution.py:284
  64.9 6.1 %collective-permute-start.11 = (bf16[56,896]{1,0:T(8,128)(2,1)S(1)}, bf16[56,896]{1,0:T(8,128)(2,1)S(1)}, u32[]{:S(2)}, u32[]{:S(2)}) collective-permute-start(bf16[56,896]{1,0:T(8,128)(2,1)S(1)} %fusion.7), channel_id=1, source_target_pairs={{0,4},{4,0},{8,12},{12,8},{1,5},{5,1},{9,13},{13,9},{2,6},{6,2},{1... | collective-permute-start | bytes 301064 | tf_op jit(solution)/shard_map/ppermute | solution.py:284
  67.5 11.1 %collective-permute-start.16 = (bf16[56,896]{1,0:T(8,128)(2,1)S(1)}, bf16[56,896]{1,0:T(8,128)(2,1)S(1)}, u32[]{:S(2)}, u32[]{:S(2)}) collective-permute-start(bf16[56,896]{1,0:T(8,128)(2,1)S(1)} %add_convert_fusion.5), channel_id=1, source_target_pairs={{0,8},{4,12},{8,0},{12,4},{1,9},{5,13},{9,1},{13,5},{2,10},{6,14},... | collective-permute-start | bytes 301064 | tf_op jit(solution)/shard_map/ppermute | solution.py:284
  71.1 11.0 %collective-permute-start.13 = (bf16[56,896]{1,0:T(8,128)(2,1)S(1)}, bf16[56,896]{1,0:T(8,128)(2,1)S(1)}, u32[]{:S(2)}, u32[]{:S(2)}) collective-permute-start(bf16[56,896]{1,0:T(8,128)(2,1)S(1)} %fusion.3), channel_id=1, source_target_pairs={{0,8},{4,12},{8,0},{12,4},{1,9},{5,13},{9,1},{13,5},{2,10},{6,14},... | collective-permute-start | bytes 301064 | tf_op jit(solution)/shard_map/ppermute | solution.py:284
  72.7 11.2 %collective-permute-start.12 = (bf16[224,256]{1,0:T(8,128)(2,1)S(1)}, bf16[224,256]{1,0:T(8,128)(2,1)S(1)}, u32[]{:S(2)}, u32[]{:S(2)}) collective-permute-start(bf16[224,256]{1,0:T(8,128)(2,1)S(1)} %get-tuple-element.62), channel_id=1, source_target_pairs={{0,8},{4,12},{8,0},{12,4},{1,9},{5,13},{9,1},{13,5},{2,10},{6,14},... | collective-permute-start | bytes 344072 | tf_op jit(solution)/shard_map/ppermute | solution.py:284
  78.6 7.3 %collective-permute-start.17 = (bf16[56,896]{1,0:T(8,128)(2,1)S(1)}, bf16[56,896]{1,0:T(8,128)(2,1)S(1)}, u32[]{:S(2)}, u32[]{:S(2)}) collective-permute-start(bf16[56,896]{1,0:T(8,128)(2,1)S(1)} %add_convert_fusion.4.refs_1_), channel_id=1, source_target_pairs={{0,4},{4,0},{8,12},{12,8},{1,5},{5,1},{9,13},{13,9},{2,6},{6,2},{1... | collective-permute-start | bytes 301064 | tf_op jit(solution)/shard_map/ppermute | solution.py:284
  82.2 4.8 %collective-permute-start.14 = (bf16[56,896]{1,0:T(8,128)(2,1)S(1)}, bf16[56,896]{1,0:T(8,128)(2,1)S(1)}, u32[]{:S(2)}, u32[]{:S(2)}) collective-permute-start(bf16[56,896]{1,0:T(8,128)(2,1)S(1)} %add_convert_fusion.6.refs_5_.refs_0_), channel_id=1, source_target_pairs={{0,4},{4,0},{8,12},{12,8},{1,5},{5,1},{9,13},{13,9},{2,6},{6,2},{1... | collective-permute-start | bytes 301064 | tf_op jit(solution)/shard_map/ppermute | solution.py:284
